TPU v7x, 32 devices: a whole 2x2x4 slice. The times are simulated.
32 devices in a mesh: grp: 2 (over x), seq: 16 (over z, y, core).
Axes of the slice: x: 2, y: 2, z: 4, core: 2. Of those that a mesh axis runs over, the one named last changes fastest.
Arguments:
- queries: bfloat16 [128, 5120], P(('grp', 'seq')), parts along dimension 0
- keys: bfloat16 [16384, 5120], P(('grp', 'seq')), parts along dimension 0
- values: bfloat16 [16384, 5120], P(('grp', 'seq')), parts along dimension 0, may hold values from -6 to 6
- gain: float32 [5120], replicated, may hold values from 0.1 to 1.9
Outputs:
- window_out: bfloat16 [128, 5120], P(('grp', 'seq')), parts along dimension 0
There are 2 independent parts, one for each index of `grp`. A program takes and returns all parts, laid end to end along the dimension named above; an argument that names none is the same for every part. Nothing has to cross between parts.
All inputs are finite; a program needn't handle non-finite values.
Results may differ from a plain program's by a relative error of at most 0.001.
Values may be sent and summed in bfloat16 or wider, within the bound.
No kernel may reach another device: no remote copies, remote signals or barrier semaphores. Data moves between devices by JAX's collectives and lax.ppermute only.
A program may use at most 128 MiB of HBM per device.

v0:
```python
import functools
import math

import jax
import jax.numpy as jnp
from jax import lax
from jax.experimental import pallas as pl
from jax.experimental.pallas import tpu as pltpu
from jax.sharding import PartitionSpec as P

HDIM = 128
EXP2_SCALE = math.log2(math.e) / math.sqrt(HDIM)
FETCH_FLOPS = 1_500_000_000
CHAINS = 2
CODE_SPAN = 250.0
VMEM_SPEC = pl.BlockSpec(memory_space=pltpu.VMEM)


def copy_kernel(source_ref, out_ref):
    out_ref[...] = source_ref[...]


def join_kernel(*refs):
    refs[-1][...] = jnp.concatenate([ref[...] for ref in refs[:-1]], axis=0)


def attend_kernel(
    query_here_ref, query_there_ref, key_ref, value_ref, keep_ref, send_ref, dots_ref, weights_ref, *, first_head
):
    half, width = query_here_ref.shape[0], keep_ref.shape[1] - 2 * HDIM
    rows = 2 * half
    heads = width // HDIM
    slots = dots_ref.shape[0]

    def shifted(head):
        return slice((first_head + head) * HDIM, (first_head + head + 1) * HDIM)

    def score(head):
        columns = shifted(head)
        dots_ref[head % slots] = lax.dot_general(
            jnp.concatenate([query_here_ref[:, columns], query_there_ref[:, columns]], axis=0),
            key_ref[:, columns],
            (((1,), (1,)), ((), ())),
            preferred_element_type=jnp.float32,
        )

    def weigh(head):
        dots = dots_ref[head % slots]
        peak = jnp.max(dots, axis=1, keepdims=True)
        weights = jnp.exp2((dots - peak) * EXP2_SCALE)
        total = jnp.sum(weights, axis=1, keepdims=True)
        coarse = weights.astype(jnp.bfloat16)
        weights_ref[head % slots, :rows] = coarse
        weights_ref[head % slots, rows:] = (weights - coarse.astype(jnp.float32)).astype(jnp.bfloat16)
        for ref, first in ((keep_ref, 0), (send_ref, half)):
            ref[:, width + head : width + head + 1] = peak[first : first + half]
            ref[:, width + HDIM + head : width + HDIM + head + 1] = total[first : first + half]

    def accumulate(head):
        columns = slice(head * HDIM, (head + 1) * HDIM)
        sums = jnp.dot(weights_ref[head % slots], value_ref[:, shifted(head)], preferred_element_type=jnp.float32)
        numerator = sums[:rows] + sums[rows:]
        keep_ref[:, columns] = numerator[:half]
        send_ref[:, columns] = numerator[half:]

    group = slots // 2
    for ref in (keep_ref, send_ref):
        ref[:, width:] = jnp.zeros((half, 2 * HDIM), jnp.float32)
    steps = heads // group
    for step in range(steps + 2):
        for member in range(group):
            for stage, lag in ((score, 0), (weigh, 1), (accumulate, 2)):
                if 0 <= step - lag < steps:
                    stage((step - lag) * group + member)


def exact_terms(values):
    first = values.astype(jnp.bfloat16).astype(jnp.float32)
    rest = values - first
    second = rest.astype(jnp.bfloat16).astype(jnp.float32)
    return first, second, rest - second


def pack_statistics(maxima, denominators, unit, heads):
    lane = lax.broadcasted_iota(jnp.int32, maxima.shape, 1)
    packed = unit
    for place, term in enumerate((*exact_terms(maxima), *exact_terms(denominators))):
        moved = term if place == 0 else pltpu.roll(term, place * heads, 1)
        packed = jnp.where((lane >= place * heads) & (lane < (place + 1) * heads), moved, packed)
    return packed.astype(jnp.bfloat16)


def unpack_statistics(packed, heads):
    terms = packed.astype(jnp.float32)
    place = [terms, *(pltpu.roll(terms, HDIM - index * heads, 1) for index in range(1, 6))]
    unit = jnp.broadcast_to(terms[:, 6 * heads : 6 * heads + 1], terms.shape)
    return place[0] + (place[1] + place[2]), place[3] + (place[4] + place[5]), unit


def read_statistics(ref, width, coded):
    if not coded:
        return ref[:, width : width + HDIM], ref[:, width + HDIM :], None
    maxima, denominators, unit = unpack_statistics(ref[:, width:], width // HDIM)
    return maxima, denominators, unit * (1.0 / CODE_SPAN)


def read_numerator(ref, columns, coded):
    if not coded:
        return ref[:, columns]
    code = ref[:, columns].astype(jnp.float32)
    size = jnp.log2(jnp.abs(code)) + CODE_SPAN / 2
    return jnp.where(code < 0, -size, size)


def combine(refs, coded, width):
    statistics = [read_statistics(ref, width, kind == "coded") for ref, kind in zip(refs, coded)]
    maxima = functools.reduce(jnp.maximum, [m for m, _, _ in statistics])
    scales = [jnp.exp2((m - maxima) * EXP2_SCALE) for m, _, _ in statistics]
    denominators = sum(scale * d for scale, (_, d, _) in zip(scales, statistics))
    inverse = 1.0 / denominators
    factors = []
    for kind, scale, (_, d, unit) in zip(coded, scales, statistics):
        factor = scale * inverse
        if kind != "sums":
            factor = factor * d
        factors.append(factor if unit is None else factor * unit)
    return maxima, denominators, factors


def combined_mean(refs, coded, factors, head):
    columns = slice(head * HDIM, (head + 1) * HDIM)
    lane = slice(head, head + 1)
    return sum(f[:, lane] * read_numerator(ref, columns, k == "coded") for ref, k, f in zip(refs, coded, factors))


def section(ref, chain, width, kind):
    stride = width + (HDIM if kind == "coded" else 2 * HDIM)
    return ref.at[:, chain * stride : (chain + 1) * stride]


def merge_kernel(*refs, kinds, chains, separate):
    count = len(kinds)
    arrays = count * chains if separate else count
    all_keep_ref, *all_send_refs = refs[arrays:-1]
    means_ref = refs[-1]
    block = all_keep_ref.shape[0]
    sent, width = means_ref.shape
    heads = width // HDIM
    for chain in range(chains):
        if separate:
            sources = refs[chain * count : (chain + 1) * count]
        else:
            sources = [section(ref, chain, width, kind) for ref, kind in zip(refs, kinds)]
        keep_ref = section(all_keep_ref, chain, width, "means")
        maxima, denominators, factors = combine(sources, kinds, width)
        largest = jnp.full((sent, HDIM), 1e-30, jnp.float32)
        for head in range(heads):
            columns = slice(head * HDIM, (head + 1) * HDIM)
            merged = combined_mean(sources, kinds, factors, head)
            keep_ref[:, columns] = merged[:block]
            means_ref[:, columns] = merged[block:]
            largest = jnp.maximum(largest, jnp.abs(merged[block:]))
        keep_ref[:, width : width + HDIM] = maxima[:block]
        keep_ref[:, width + HDIM :] = denominators[:block]
        unit = jnp.broadcast_to(jnp.max(largest, axis=1, keepdims=True), largest.shape)
        unit = (unit * 1.01).astype(jnp.bfloat16).astype(jnp.float32)
        step = CODE_SPAN / unit
        statistics = pack_statistics(maxima[block:], denominators[block:], unit, heads)
        for index, all_send_ref in enumerate(all_send_refs):
            rows = slice(index * block, (index + 1) * block)
            send_ref = section(all_send_ref, chain, width, "coded")
            send_ref[:, width:] = statistics[rows]
            for head in range(heads):
                columns = slice(head * HDIM, (head + 1) * HDIM)
                mean = means_ref[rows, columns]
                code = jnp.exp2(jnp.abs(mean) * step[rows] - CODE_SPAN / 2)
                send_ref[:, columns] = jnp.where(mean < 0, -code, code).astype(jnp.bfloat16)


def finish_kernel(*refs, kinds, chains):
    gain_ref, out_ref = refs[-2:]
    rows, all_width = out_ref.shape
    width = all_width // chains
    squares = jnp.zeros((rows, HDIM), jnp.float32)
    attended = []
    for chain in range(chains):
        sources = [section(ref, chain, width, kind) for ref, kind in zip(refs, kinds)]
        _, _, factors = combine(sources, kinds, width)
        for head in range(width // HDIM):
            block = combined_mean(sources, kinds, factors, head)
            squares = squares + block * block
            attended.append(block)
    mean = jnp.sum(squares, axis=1, keepdims=True) / all_width
    inverse = 1.0 / jnp.sqrt(mean + 1e-06)
    for head, block in enumerate(attended):
        columns = slice(head * HDIM, (head + 1) * HDIM)
        out_ref[:, columns] = (block * inverse * gain_ref[:, columns]).astype(out_ref.dtype)


def call(kernel, out_shape, operands, flops=0, scratch=(), limit=4 << 20):
    outs = out_shape if isinstance(out_shape, (tuple, list)) else [out_shape]
    size = sum(math.prod(a.shape) * a.dtype.itemsize for a in (*operands, *outs))
    return pl.pallas_call(
        kernel,
        out_shape=out_shape,
        in_specs=[VMEM_SPEC] * len(operands),
        out_specs=jax.tree.map(lambda _: VMEM_SPEC, out_shape),
        scratch_shapes=scratch,
        cost_estimate=pl.CostEstimate(flops=flops, bytes_accessed=size, transcendentals=0),
        compiler_params=pltpu.CompilerParams(vmem_limit_bytes=limit),
    )(*operands)


def exchange(array, mask):
    return lax.ppermute(array, "seq", [(i, i ^ mask) for i in range(lax.axis_size("seq"))])


def chip_stages(peers):
    bits = [1 << bit for bit in range(1, peers.bit_length() - 1)]
    square = [bits[:1], [*bits[:2], sum(bits[:2])]][len(bits) > 2]
    return [[mask ^ 1 for mask in masks] for masks in (square, *([bit] for bit in bits[len(square).bit_length() :]))]


def shards(queries, keys, values, gain):
    stages = chip_stages(lax.axis_size("seq"))
    core = 1
    rows, width = queries.shape
    part = width // CHAINS
    tokens = keys.shape[0]
    gain = call(copy_kernel, jax.ShapeDtypeStruct((1, width), gain.dtype), [gain.reshape(1, width)], FETCH_FLOPS)

    window = queries
    for masks in reversed(stages):
        pieces = [window, *(exchange(window, mask) for mask in masks)]
        shape = jax.ShapeDtypeStruct((len(pieces) * window.shape[0], width), window.dtype)
        window = call(join_kernel, shape, pieces, FETCH_FLOPS)
    arrived = exchange(window, core)
    count = window.shape[0]

    plain = lambda count, parts: jax.ShapeDtypeStruct((count, parts * (part + 2 * HDIM)), jnp.float32)
    code = lambda count: jax.ShapeDtypeStruct((count, CHAINS * (part + HDIM)), jnp.bfloat16)

    sources = []
    for chain in range(CHAINS):
        keep, send = call(
            functools.partial(attend_kernel, first_head=chain * part // HDIM),
            (plain(count, 1), plain(count, 1)),
            (window, arrived, keys, values),
            8 * count * tokens * part,
            [pltpu.VMEM((4, 2 * count, tokens), jnp.float32), pltpu.VMEM((4, 4 * count, tokens), jnp.bfloat16)],
            16 << 20,
        )
        sources += [keep, exchange(send, core)]
    kinds, separate = ("sums", "sums"), True
    for masks in stages:
        block = count // (len(masks) + 1)
        keep, *sends = call(
            functools.partial(merge_kernel, kinds=kinds, chains=CHAINS, separate=separate),
            (plain(block, CHAINS), *[code(block)] * len(masks)),
            sources,
            0,
            [pltpu.VMEM((count - block, part), jnp.float32)],
        )
        sources = [keep, *(exchange(send, mask) for send, mask in zip(sends, masks))]
        kinds, separate, count = ("means", *["coded"] * len(masks)), False, block
    kernel = functools.partial(finish_kernel, kinds=kinds, chains=CHAINS)
    return call(kernel, jax.ShapeDtypeStruct((rows, width), jnp.bfloat16), (*sources, gain), 0)


def solution(mesh):
    spec = P(("grp", "seq"), None)
    return jax.shard_map(shards, mesh=mesh, in_specs=(spec, spec, spec, P()), out_specs=spec, check_vma=False)
```

profile of v0, /device:TPU:0, one launch (start us, length us, event | category | flops | bytes accessed | tf_op | source)
XLA Modules:
  0.0 39.6 jit_solution(9780216369526432418)
XLA Ops:
  0.0 3.5 %collective-permute-start = (bf16[4,5120]{1,0:T(4,128)(2,1)}, bf16[4,5120]{1,0:T(4,128)(2,1)S(1)}, u32[]{:S(2)}, u32[]{:S(2)}) collective-permute-start(bf16[4,5120]{1,0:T(4,128)(2,1)} %refs_0_.1), channel_id=1, source_target_pairs={{0,9},{1,8},{2,11},{3,10},{4,13},{5,12},{6,15},{7,14},{8,1},{9,0},... | collective-permute-start | bytes 122888 | tf_op jit(solution)/shard_map/ppermute | solution.py:215
  3.5 2.3 %collective-permute-done.refs_1_ = bf16[4,5120]{1,0:T(4,128)(2,1)S(1)} collective-permute-done((bf16[4,5120]{1,0:T(4,128)(2,1)}, bf16[4,5120]{1,0:T(4,128)(2,1)S(1)}, u32[]{:S(2)}, u32[]{:S(2)}) %collective-permute-start) | collective-permute-done | bytes 40992 | tf_op jit(solution)/shard_map/ppermute | solution.py:215
  5.8 0.8 %copy-done.2 = bf16[4,5120]{1,0:T(4,128)(2,1)S(1)} copy-done((bf16[4,5120]{1,0:T(4,128)(2,1)S(1)}, bf16[4,5120]{1,0:T(4,128)(2,1)}, u32[]{:S(2)}) %copy-start.2) | copy-done | bytes 40984
  6.6 1.7 %collective-permute-start.1 = (bf16[8,5120]{1,0:T(8,128)(2,1)S(1)}, bf16[8,5120]{1,0:T(8,128)(2,1)S(1)}, u32[]{:S(2)}, u32[]{:S(2)}) collective-permute-start(bf16[8,5120]{1,0:T(8,128)(2,1)S(1)} %shard_map.46.refs_0_), channel_id=1, source_target_pairs={{0,3},{1,2},{2,1},{3,0},{4,7},{5,6},{6,5},{7,4},{8,11},{9,10},{10,... | collective-permute-start | bytes 245768 | tf_op jit(solution)/shard_map/ppermute | solution.py:215
  8.3 1.8 %collective-permute-start.2 = (bf16[8,5120]{1,0:T(8,128)(2,1)S(1)}, bf16[8,5120]{1,0:T(8,128)(2,1)S(1)}, u32[]{:S(2)}, u32[]{:S(2)}) collective-permute-start(bf16[8,5120]{1,0:T(8,128)(2,1)S(1)} %shard_map.46.refs_0_), channel_id=1, source_target_pairs={{0,5},{1,4},{2,7},{3,6},{4,1},{5,0},{6,3},{7,2},{8,13},{9,12},{10,... | collective-permute-start | bytes 245768 | tf_op jit(solution)/shard_map/ppermute | solution.py:215
  10.1 0.8 %collective-permute-done.1.refs_1_ = bf16[8,5120]{1,0:T(8,128)(2,1)S(1)} collective-permute-done((bf16[8,5120]{1,0:T(8,128)(2,1)S(1)}, bf16[8,5120]{1,0:T(8,128)(2,1)S(1)}, u32[]{:S(2)}, u32[]{:S(2)}) %collective-permute-start.1) | collective-permute-done | bytes 81952 | tf_op jit(solution)/shard_map/ppermute | solution.py:215
  10.9 2.0 %collective-permute-done.2.refs_2_ = bf16[8,5120]{1,0:T(8,128)(2,1)S(1)} collective-permute-done((bf16[8,5120]{1,0:T(8,128)(2,1)S(1)}, bf16[8,5120]{1,0:T(8,128)(2,1)S(1)}, u32[]{:S(2)}, u32[]{:S(2)}) %collective-permute-start.2) | collective-permute-done | bytes 81952 | tf_op jit(solution)/shard_map/ppermute | solution.py:215
  12.9 2.4 %collective-permute-done.3.refs_3_ = bf16[8,5120]{1,0:T(8,128)(2,1)S(1)} collective-permute-done((bf16[8,5120]{1,0:T(8,128)(2,1)S(1)}, bf16[8,5120]{1,0:T(8,128)(2,1)S(1)}, u32[]{:S(2)}, u32[]{:S(2)}) %collective-permute-start.3) | collective-permute-done | bytes 81952 | tf_op jit(solution)/shard_map/ppermute | solution.py:215
  15.3 0.3 collective-permute-start.4
  15.7 1.4 %collective-permute-done.4.query_there_ref = bf16[32,5120]{1,0:T(8,128)(2,1)S(1)} collective-permute-done((bf16[32,5120]{1,0:T(8,128)(2,1)S(1)}, bf16[32,5120]{1,0:T(8,128)(2,1)S(1)}, u32[]{:S(2)}, u32[]{:S(2)}) %collective-permute-start.4) | collective-permute-done | bytes 327712 | tf_op jit(solution)/shard_map/ppermute | solution.py:215
  17.0 1.9 %shard_map.49 = (f32[32,2816]{1,0:T(8,128)S(1)}, f32[32,2816]{1,0:T(8,128)S(1)}) custom-call(bf16[32,5120]{1,0:T(8,128)(2,1)S(1)} %shard_map.47.query_here_ref, bf16[32,5120]{1,0:T(8,128)(2,1)S(1)} %collective-permute-done.4.query_there_ref, bf16[512,5120]{1,0:T(8,128)(2,1)S(1)} %copy-done, bf16[512,5120]{1,0:T(8,128)(2,1)S(1)} %copy-done.1), custom_call_target="tpu_custom_call" | custom-call | flops 335544320 | bytes 11862016 | tf_op jit(solution)/shard_map/pallas_call | solution.py:203
  19.3 1.9 %shard_map.48 = (f32[32,2816]{1,0:T(8,128)S(1)}, f32[32,2816]{1,0:T(8,128)S(1)}) custom-call(bf16[32,5120]{1,0:T(8,128)(2,1)S(1)} %shard_map.47.query_here_ref, bf16[32,5120]{1,0:T(8,128)(2,1)S(1)} %collective-permute-done.4.query_there_ref, bf16[512,5120]{1,0:T(8,128)(2,1)S(1)} %copy-done, bf16[512,5120]{1,0:T(8,128)(2,1)S(1)} %copy-done.1), custom_call_target="tpu_custom_call" | custom-call | flops 335544320 | bytes 11862016 | tf_op jit(solution)/shard_map/pallas_call | solution.py:203
  21.5 1.4 %collective-permute-done.5.refs_1_ = f32[32,2816]{1,0:T(8,128)S(1)} collective-permute-done((f32[32,2816]{1,0:T(8,128)S(1)}, f32[32,2816]{1,0:T(8,128)S(1)}, u32[]{:S(2)}, u32[]{:S(2)}) %collective-permute-start.5) | collective-permute-done | bytes 360480 | tf_op jit(solution)/shard_map/ppermute | solution.py:215
  23.0 0.8 %shard_map.50 = (f32[8,5632]{1,0:T(8,128)S(1)}, bf16[8,5376]{1,0:T(8,128)(2,1)S(1)}, bf16[8,5376]{1,0:T(8,128)(2,1)S(1)}, bf16[8,5376]{1,0:T(8,128)(2,1)S(1)}) custom-call(f32[32,2816]{1,0:T(8,128)S(1)} %get-tuple-element.15.refs_0_, f32[32,2816]{1,0:T(8,128)S(1)} %collective-permute-done.5.refs_1_, f32[32,2816]{1,0:T(8,128)S(1)} %get-tuple-element.17.refs_2_, ...), custom_call_target="tpu_custom_call" | custom-call | bytes 1880064 | tf_op jit(solution)/shard_map/pallas_call | solution.py:203
  23.7 0.6 %collective-permute-start.7 = (bf16[8,5376]{1,0:T(8,128)(2,1)S(1)}, bf16[8,5376]{1,0:T(8,128)(2,1)S(1)}, u32[]{:S(2)}, u32[]{:S(2)}) collective-permute-start(bf16[8,5376]{1,0:T(8,128)(2,1)S(1)} %get-tuple-element.20), channel_id=1, source_target_pairs={{0,3},{1,2},{2,1},{3,0},{4,7},{5,6},{6,5},{7,4},{8,11},{9,10},{10,... | collective-permute-start | bytes 258056 | tf_op jit(solution)/shard_map/ppermute | solution.py:215
  24.3 1.7 %collective-permute-start.8 = (bf16[8,5376]{1,0:T(8,128)(2,1)S(1)}, bf16[8,5376]{1,0:T(8,128)(2,1)S(1)}, u32[]{:S(2)}, u32[]{:S(2)}) collective-permute-start(bf16[8,5376]{1,0:T(8,128)(2,1)S(1)} %get-tuple-element.21), channel_id=1, source_target_pairs={{0,5},{1,4},{2,7},{3,6},{4,1},{5,0},{6,3},{7,2},{8,13},{9,12},{10,... | collective-permute-start | bytes 258056 | tf_op jit(solution)/shard_map/ppermute | solution.py:215
  26.0 0.9 %collective-permute-start.9 = (bf16[8,5376]{1,0:T(8,128)(2,1)S(1)}, bf16[8,5376]{1,0:T(8,128)(2,1)S(1)}, u32[]{:S(2)}, u32[]{:S(2)}) collective-permute-start(bf16[8,5376]{1,0:T(8,128)(2,1)S(1)} %get-tuple-element.22), channel_id=1, source_target_pairs={{0,7},{1,6},{2,5},{3,4},{4,3},{5,2},{6,1},{7,0},{8,15},{9,14},{10,... | collective-permute-start | bytes 258056 | tf_op jit(solution)/shard_map/ppermute | solution.py:215
  26.9 1.3 %collective-permute-done.7.refs_1_ = bf16[8,5376]{1,0:T(8,128)(2,1)S(1)} collective-permute-done((bf16[8,5376]{1,0:T(8,128)(2,1)S(1)}, bf16[8,5376]{1,0:T(8,128)(2,1)S(1)}, u32[]{:S(2)}, u32[]{:S(2)}) %collective-permute-start.7) | collective-permute-done | bytes 86048 | tf_op jit(solution)/shard_map/ppermute | solution.py:215
  28.2 0.7 %collective-permute-done.8.refs_2_ = bf16[8,5376]{1,0:T(8,128)(2,1)S(1)} collective-permute-done((bf16[8,5376]{1,0:T(8,128)(2,1)S(1)}, bf16[8,5376]{1,0:T(8,128)(2,1)S(1)}, u32[]{:S(2)}, u32[]{:S(2)}) %collective-permute-start.8) | collective-permute-done | bytes 86048 | tf_op jit(solution)/shard_map/ppermute | solution.py:215
  28.9 2.5 %collective-permute-done.9.refs_3_ = bf16[8,5376]{1,0:T(8,128)(2,1)S(1)} collective-permute-done((bf16[8,5376]{1,0:T(8,128)(2,1)S(1)}, bf16[8,5376]{1,0:T(8,128)(2,1)S(1)}, u32[]{:S(2)}, u32[]{:S(2)}) %collective-permute-start.9) | collective-permute-done | bytes 86048 | tf_op jit(solution)/shard_map/ppermute | solution.py:215
  31.4 0.7 %shard_map.51 = (f32[4,5632]{1,0:T(4,128)S(1)}, bf16[4,5376]{1,0:T(4,128)(2,1)S(1)}) custom-call(f32[8,5632]{1,0:T(8,128)S(1)} %get-tuple-element.19.refs_0_, bf16[8,5376]{1,0:T(8,128)(2,1)S(1)} %collective-permute-done.7.refs_1_, bf16[8,5376]{1,0:T(8,128)(2,1)S(1)} %collective-permute-done.8.refs_2_, bf16[8,5376]{1,0:T(8,128)(2,1)S(1)} %collective-permute-done.9.refs_3_), custom_call_target="tpu_custom_call" | custom-call | bytes 571392 | tf_op jit(solution)/shard_map/pallas_call | solution.py:203
  32.1 3.4 %collective-permute-start.10 = (bf16[4,5376]{1,0:T(4,128)(2,1)S(1)}, bf16[4,5376]{1,0:T(4,128)(2,1)S(1)}, u32[]{:S(2)}, u32[]{:S(2)}) collective-permute-start(bf16[4,5376]{1,0:T(4,128)(2,1)S(1)} %get-tuple-element.24), channel_id=1, source_target_pairs={{0,9},{1,8},{2,11},{3,10},{4,13},{5,12},{6,15},{7,14},{8,1},{9,0},... | collective-permute-start | bytes 129032 | tf_op jit(solution)/shard_map/ppermute | solution.py:215
  35.6 3.0 %collective-permute-done.10.refs_1_ = bf16[4,5376]{1,0:T(4,128)(2,1)S(1)} collective-permute-done((bf16[4,5376]{1,0:T(4,128)(2,1)S(1)}, bf16[4,5376]{1,0:T(4,128)(2,1)S(1)}, u32[]{:S(2)}, u32[]{:S(2)}) %collective-permute-start.10) | collective-permute-done | bytes 43040 | tf_op jit(solution)/shard_map/ppermute | solution.py:215
  38.6 1.0 %shard_map.53 = bf16[4,5120]{1,0:T(4,128)(2,1)} custom-call(f32[4,5632]{1,0:T(4,128)S(1)} %get-tuple-element.23.refs_0_, bf16[4,5376]{1,0:T(4,128)(2,1)S(1)} %collective-permute-done.10.refs_1_, f32[1,5120]{1,0:T(1,128)S(1)} %shard_map.52.refs_2_), custom_call_target="tpu_custom_call" | custom-call | bytes 194560 | tf_op jit(solution)/shard_map/pallas_call | solution.py:203
  (14 shorter events, 0.7 us)
Async XLA Ops:
  0.0 17.0 %copy-start = (bf16[512,5120]{1,0:T(8,128)(2,1)S(1)}, bf16[512,5120]{1,0:T(8,128)(2,1)}, u32[]{:S(2)}) copy-start(bf16[512,5120]{1,0:T(8,128)(2,1)} %key_ref.3) | copy-start | bytes 15728644
  0.0 17.0 %copy-start.1 = (bf16[512,5120]{1,0:T(8,128)(2,1)S(1)}, bf16[512,5120]{1,0:T(8,128)(2,1)}, u32[]{:S(2)}) copy-start(bf16[512,5120]{1,0:T(8,128)(2,1)} %value_ref.3) | copy-start | bytes 15728644
  0.0 5.8 %collective-permute-start = (bf16[4,5120]{1,0:T(4,128)(2,1)}, bf16[4,5120]{1,0:T(4,128)(2,1)S(1)}, u32[]{:S(2)}, u32[]{:S(2)}) collective-permute-start(bf16[4,5120]{1,0:T(4,128)(2,1)} %refs_0_.1), channel_id=1, source_target_pairs={{0,9},{1,8},{2,11},{3,10},{4,13},{5,12},{6,15},{7,14},{8,1},{9,0},... | collective-permute-start | bytes 122888 | tf_op jit(solution)/shard_map/ppermute | solution.py:215
  5.8 0.8 %copy-start.2 = (bf16[4,5120]{1,0:T(4,128)(2,1)S(1)}, bf16[4,5120]{1,0:T(4,128)(2,1)}, u32[]{:S(2)}) copy-start(bf16[4,5120]{1,0:T(4,128)(2,1)} %refs_0_.1) | copy-start | bytes 122884
  6.6 4.3 %collective-permute-start.1 = (bf16[8,5120]{1,0:T(8,128)(2,1)S(1)}, bf16[8,5120]{1,0:T(8,128)(2,1)S(1)}, u32[]{:S(2)}, u32[]{:S(2)}) collective-permute-start(bf16[8,5120]{1,0:T(8,128)(2,1)S(1)} %shard_map.46.refs_0_), channel_id=1, source_target_pairs={{0,3},{1,2},{2,1},{3,0},{4,7},{5,6},{6,5},{7,4},{8,11},{9,10},{10,... | collective-permute-start | bytes 245768 | tf_op jit(solution)/shard_map/ppermute | solution.py:215
  8.3 4.6 %collective-permute-start.2 = (bf16[8,5120]{1,0:T(8,128)(2,1)S(1)}, bf16[8,5120]{1,0:T(8,128)(2,1)S(1)}, u32[]{:S(2)}, u32[]{:S(2)}) collective-permute-start(bf16[8,5120]{1,0:T(8,128)(2,1)S(1)} %shard_map.46.refs_0_), channel_id=1, source_target_pairs={{0,5},{1,4},{2,7},{3,6},{4,1},{5,0},{6,3},{7,2},{8,13},{9,12},{10,... | collective-permute-start | bytes 245768 | tf_op jit(solution)/shard_map/ppermute | solution.py:215
  10.1 5.2 %collective-permute-start.3 = (bf16[8,5120]{1,0:T(8,128)(2,1)S(1)}, bf16[8,5120]{1,0:T(8,128)(2,1)S(1)}, u32[]{:S(2)}, u32[]{:S(2)}) collective-permute-start(bf16[8,5120]{1,0:T(8,128)(2,1)S(1)} %shard_map.46.refs_0_), channel_id=1, source_target_pairs={{0,7},{1,6},{2,5},{3,4},{4,3},{5,2},{6,1},{7,0},{8,15},{9,14},{10,... | collective-permute-start | bytes 245768 | tf_op jit(solution)/shard_map/ppermute | solution.py:215
  15.3 1.7 %collective-permute-start.4 = (bf16[32,5120]{1,0:T(8,128)(2,1)S(1)}, bf16[32,5120]{1,0:T(8,128)(2,1)S(1)}, u32[]{:S(2)}, u32[]{:S(2)}) collective-permute-start(bf16[32,5120]{1,0:T(8,128)(2,1)S(1)} %shard_map.47.query_here_ref), channel_id=1, source_target_pairs={{0,1},{1,0},{2,3},{3,2},{4,5},{5,4},{6,7},{7,6},{8,9},{9,8},{10,11... | collective-permute-start | bytes 983048 | tf_op jit(solution)/shard_map/ppermute | solution.py:215
  18.9 16.6 %copy-start.3 = (f32[5120]{0:T(1024)S(1)}, f32[5120]{0:T(1024)}, u32[]{:S(2)}) copy-start(f32[5120]{0:T(1024)} %param.7) | copy-start | bytes 61444
  19.0 2.6 %collective-permute-start.6 = (f32[32,2816]{1,0:T(8,128)S(1)}, f32[32,2816]{1,0:T(8,128)S(1)}, u32[]{:S(2)}, u32[]{:S(2)}) collective-permute-start(f32[32,2816]{1,0:T(8,128)S(1)} %get-tuple-element.18), channel_id=1, source_target_pairs={{0,1},{1,0},{2,3},{3,2},{4,5},{5,4},{6,7},{7,6},{8,9},{9,8},{10,11... | collective-permute-start | bytes 1081352 | tf_op jit(solution)/shard_map/ppermute | solution.py:215
  21.2 1.7 %collective-permute-start.5 = (f32[32,2816]{1,0:T(8,128)S(1)}, f32[32,2816]{1,0:T(8,128)S(1)}, u32[]{:S(2)}, u32[]{:S(2)}) collective-permute-start(f32[32,2816]{1,0:T(8,128)S(1)} %get-tuple-element.16), channel_id=1, source_target_pairs={{0,1},{1,0},{2,3},{3,2},{4,5},{5,4},{6,7},{7,6},{8,9},{9,8},{10,11... | collective-permute-start | bytes 1081352 | tf_op jit(solution)/shard_map/ppermute | solution.py:215
  23.7 4.5 %collective-permute-start.7 = (bf16[8,5376]{1,0:T(8,128)(2,1)S(1)}, bf16[8,5376]{1,0:T(8,128)(2,1)S(1)}, u32[]{:S(2)}, u32[]{:S(2)}) collective-permute-start(bf16[8,5376]{1,0:T(8,128)(2,1)S(1)} %get-tuple-element.20), channel_id=1, source_target_pairs={{0,3},{1,2},{2,1},{3,0},{4,7},{5,6},{6,5},{7,4},{8,11},{9,10},{10,... | collective-permute-start | bytes 258056 | tf_op jit(solution)/shard_map/ppermute | solution.py:215
  24.3 4.6 %collective-permute-start.8 = (bf16[8,5376]{1,0:T(8,128)(2,1)S(1)}, bf16[8,5376]{1,0:T(8,128)(2,1)S(1)}, u32[]{:S(2)}, u32[]{:S(2)}) collective-permute-start(bf16[8,5376]{1,0:T(8,128)(2,1)S(1)} %get-tuple-element.21), channel_id=1, source_target_pairs={{0,5},{1,4},{2,7},{3,6},{4,1},{5,0},{6,3},{7,2},{8,13},{9,12},{10,... | collective-permute-start | bytes 258056 | tf_op jit(solution)/shard_map/ppermute | solution.py:215
  26.0 5.4 %collective-permute-start.9 = (bf16[8,5376]{1,0:T(8,128)(2,1)S(1)}, bf16[8,5376]{1,0:T(8,128)(2,1)S(1)}, u32[]{:S(2)}, u32[]{:S(2)}) collective-permute-start(bf16[8,5376]{1,0:T(8,128)(2,1)S(1)} %get-tuple-element.22), channel_id=1, source_target_pairs={{0,7},{1,6},{2,5},{3,4},{4,3},{5,2},{6,1},{7,0},{8,15},{9,14},{10,... | collective-permute-start | bytes 258056 | tf_op jit(solution)/shard_map/ppermute | solution.py:215
  32.1 6.4 %collective-permute-start.10 = (bf16[4,5376]{1,0:T(4,128)(2,1)S(1)}, bf16[4,5376]{1,0:T(4,128)(2,1)S(1)}, u32[]{:S(2)}, u32[]{:S(2)}) collective-permute-start(bf16[4,5376]{1,0:T(4,128)(2,1)S(1)} %get-tuple-element.24), channel_id=1, source_target_pairs={{0,9},{1,8},{2,11},{3,10},{4,13},{5,12},{6,15},{7,14},{8,1},{9,0},... | collective-permute-start | bytes 129032 | tf_op jit(solution)/shard_map/ppermute | solution.py:215
where the time goes:
time: 39.8 us; the launch traced here: 39.6 us
  waiting for transfers between devices  17.8 us (45%)
  starting transfers between devices  14.5 us (36%)
  Pallas kernels  6.4 us (16%)
  local copies, waits for them, and re-layouts  0.79 us (2%)
    ppermute x11, waiting for transfers between devices, exchange(): lax.ppermute(array, 'seq', [(i, i ^ mask) for i in range(lax.axis_size('s...  17.8 us
    ppermute x11, starting transfers between devices, exchange(): lax.ppermute(array, 'seq', [(i, i ^ mask) for i in range(lax.axis_size('s...  14.5 us
    pallas_call x8, Pallas kernels, call(): pl.pallas_call(kernel, out_shape=out_shape, in_specs=[VMEM_SPEC] * len(op...  6.4 us
  transfers between devices with their start and end apart: 11, of which 10 were waited for; matrix products, arithmetic and copies ran while one was open for 0% of the time, Pallas kernels for 5%

commit v1 on v0

--- a/solution.py
+++ b/solution.py
@@ -138,41 +138,37 @@
     return ref.at[:, chain * stride : (chain + 1) * stride]
 
 
-def merge_kernel(*refs, kinds, chains, separate):
-    count = len(kinds)
-    arrays = count * chains if separate else count
-    all_keep_ref, *all_send_refs = refs[arrays:-1]
+def merge_kernel(*refs, kinds, chains, results):
+    all_keep_ref, *all_send_refs = refs[-1 - results : -1]
     means_ref = refs[-1]
     block = all_keep_ref.shape[0]
-    sent, width = means_ref.shape
+    sent, width = means_ref.shape[0], means_ref.shape[1] // len(chains)
     heads = width // HDIM
-    for chain in range(chains):
-        if separate:
-            sources = refs[chain * count : (chain + 1) * count]
-        else:
-            sources = [section(ref, chain, width, kind) for ref, kind in zip(refs, kinds)]
-        keep_ref = section(all_keep_ref, chain, width, "means")
-        maxima, denominators, factors = combine(sources, kinds, width)
+    sources = [[section(ref, i, width, k) for ref, k in zip(refs, kinds)] for i in range(len(chains))]
+    keeps = [section(all_keep_ref, chain, width, "means") for chain in chains]
+    combined = [combine(group, kinds, width) for group in sources]
+    steps = []
+    for index, (group, keep_ref, (maxima, denominators, factors)) in enumerate(zip(sources, keeps, combined)):
         largest = jnp.full((sent, HDIM), 1e-30, jnp.float32)
         for head in range(heads):
             columns = slice(head * HDIM, (head + 1) * HDIM)
-            merged = combined_mean(sources, kinds, factors, head)
+            merged = combined_mean(group, kinds, factors, head)
             keep_ref[:, columns] = merged[:block]
-            means_ref[:, columns] = merged[block:]
+            means_ref[:, index * width + head * HDIM : index * width + (head + 1) * HDIM] = merged[block:]
             largest = jnp.maximum(largest, jnp.abs(merged[block:]))
         keep_ref[:, width : width + HDIM] = maxima[:block]
         keep_ref[:, width + HDIM :] = denominators[:block]
         unit = jnp.broadcast_to(jnp.max(largest, axis=1, keepdims=True), largest.shape)
         unit = (unit * 1.01).astype(jnp.bfloat16).astype(jnp.float32)
-        step = CODE_SPAN / unit
-        statistics = pack_statistics(maxima[block:], denominators[block:], unit, heads)
-        for index, all_send_ref in enumerate(all_send_refs):
-            rows = slice(index * block, (index + 1) * block)
+        steps.append((CODE_SPAN / unit, pack_statistics(maxima[block:], denominators[block:], unit, heads)))
+    for index, (chain, (step, statistics)) in enumerate(zip(chains, steps)):
+        for place, all_send_ref in enumerate(all_send_refs):
+            rows = slice(place * block, (place + 1) * block)
             send_ref = section(all_send_ref, chain, width, "coded")
             send_ref[:, width:] = statistics[rows]
             for head in range(heads):
                 columns = slice(head * HDIM, (head + 1) * HDIM)
-                mean = means_ref[rows, columns]
+                mean = means_ref[rows, index * width + head * HDIM : index * width + (head + 1) * HDIM]
                 code = jnp.exp2(jnp.abs(mean) * step[rows] - CODE_SPAN / 2)
                 send_ref[:, columns] = jnp.where(mean < 0, -code, code).astype(jnp.bfloat16)
 
@@ -181,15 +177,16 @@
     gain_ref, out_ref = refs[-2:]
     rows, all_width = out_ref.shape
     width = all_width // chains
-    squares = jnp.zeros((rows, HDIM), jnp.float32)
+    sources = [[section(ref, chain, width, k) for ref, k in zip(refs, kinds)] for chain in range(chains)]
+    combined = [combine(group, kinds, width) for group in sources]
+    squares = [jnp.zeros((rows, HDIM), jnp.float32)] * 4
     attended = []
-    for chain in range(chains):
-        sources = [section(ref, chain, width, kind) for ref, kind in zip(refs, kinds)]
-        _, _, factors = combine(sources, kinds, width)
+    for group, (_, _, factors) in zip(sources, combined):
         for head in range(width // HDIM):
-            block = combined_mean(sources, kinds, factors, head)
-            squares = squares + block * block
+            block = combined_mean(group, kinds, factors, head)
+            squares[head % 4] = squares[head % 4] + block * block
             attended.append(block)
+    squares = sum(squares)
     mean = jnp.sum(squares, axis=1, keepdims=True) / all_width
     inverse = 1.0 / jnp.sqrt(mean + 1e-06)
     for head, block in enumerate(attended):
@@ -197,7 +194,7 @@
         out_ref[:, columns] = (block * inverse * gain_ref[:, columns]).astype(out_ref.dtype)
 
 
-def call(kernel, out_shape, operands, flops=0, scratch=(), limit=4 << 20):
+def call(kernel, out_shape, operands, flops=0, scratch=(), limit=4 << 20, aliases={}):
     outs = out_shape if isinstance(out_shape, (tuple, list)) else [out_shape]
     size = sum(math.prod(a.shape) * a.dtype.itemsize for a in (*operands, *outs))
     return pl.pallas_call(
@@ -206,6 +203,7 @@
         in_specs=[VMEM_SPEC] * len(operands),
         out_specs=jax.tree.map(lambda _: VMEM_SPEC, out_shape),
         scratch_shapes=scratch,
+        input_output_aliases=aliases,
         cost_estimate=pl.CostEstimate(flops=flops, bytes_accessed=size, transcendentals=0),
         compiler_params=pltpu.CompilerParams(vmem_limit_bytes=limit),
     )(*operands)
@@ -217,8 +215,8 @@
 
 def chip_stages(peers):
     bits = [1 << bit for bit in range(1, peers.bit_length() - 1)]
-    square = [bits[:1], [*bits[:2], sum(bits[:2])]][len(bits) > 2]
-    return [[mask ^ 1 for mask in masks] for masks in (square, *([bit] for bit in bits[len(square).bit_length() :]))]
+    square = [bits[:1], [sum(bits[:2]), *bits[:2]]][len(bits) > 2]
+    return [square, *([bit] for bit in bits[len(square).bit_length() :])]
 
 
 def shards(queries, keys, values, gain):
@@ -240,7 +238,18 @@
     plain = lambda count, parts: jax.ShapeDtypeStruct((count, parts * (part + 2 * HDIM)), jnp.float32)
     code = lambda count: jax.ShapeDtypeStruct((count, CHAINS * (part + HDIM)), jnp.bfloat16)
 
-    sources = []
+    def merge(sources, kinds, masks, block, chains, before):
+        shapes = (plain(block, CHAINS), *[code(block)] * len(masks))
+        return call(
+            functools.partial(merge_kernel, kinds=kinds, chains=chains, results=len(shapes)),
+            shapes,
+            (*sources, *before),
+            0,
+            [pltpu.VMEM((block * len(masks), part * len(chains)), jnp.float32)],
+            aliases={len(sources) + place: place for place in range(len(before))},
+        )
+
+    partials = []
     for chain in range(CHAINS):
         keep, send = call(
             functools.partial(attend_kernel, first_head=chain * part // HDIM),
@@ -250,19 +259,19 @@
             [pltpu.VMEM((4, 2 * count, tokens), jnp.float32), pltpu.VMEM((4, 4 * count, tokens), jnp.bfloat16)],
             16 << 20,
         )
-        sources += [keep, exchange(send, core)]
-    kinds, separate = ("sums", "sums"), True
+        partials.append((keep, exchange(send, core)))
     for masks in stages:
-        block = count // (len(masks) + 1)
-        keep, *sends = call(
-            functools.partial(merge_kernel, kinds=kinds, chains=CHAINS, separate=separate),
-            (plain(block, CHAINS), *[code(block)] * len(masks)),
-            sources,
-            0,
-            [pltpu.VMEM((count - block, part), jnp.float32)],
-        )
+        count = count // (len(masks) + 1)
+        if partials is not None:
+            merged = ()
+            for chain, pair in enumerate(partials):
+                merged = merge(pair, ("sums", "sums"), masks, count, (chain,), merged)
+            partials = None
+        else:
+            merged = merge(sources, kinds, masks, count, tuple(range(CHAINS)), ())
+        keep, *sends = merged
         sources = [keep, *(exchange(send, mask) for send, mask in zip(sends, masks))]
-        kinds, separate, count = ("means", *["coded"] * len(masks)), False, block
+        kinds = ("means", *["coded"] * len(masks))
     kernel = functools.partial(finish_kernel, kinds=kinds, chains=CHAINS)
     return call(kernel, jax.ShapeDtypeStruct((rows, width), jnp.bfloat16), (*sources, gain), 0)
 

time: 39.8 us -> 37.9 us (0.952)
  waiting for transfers between devices: 17.8 us -> 15.6 us
  starting transfers between devices: 14.5 us -> 14.9 us
    ppermute x11, waiting for transfers between devices: 17.8 us -> 15.6 us  [exchange(): lax.ppermute(array, 'seq', [(i, i ^ mask) for i in range(lax.axis_size('s...]
    pallas_call x8 -> x9, Pallas kernels: 6.4 us -> 6.34 us  [call(): pl.pallas_call(kernel, out_shape=out_shape, in_specs=[VMEM_SPEC] * len(op...]
  transfers between devices with their start and end apart: 11 -> 11, of which waited for: 10 -> 10; matrix products, arithmetic and copies ran while one was open for 0% -> 0% of each run, Pallas kernels for 5% -> 6%
where the time goes in v1:
time: 37.9 us; the launch traced here: 37.7 us
  waiting for transfers between devices  15.6 us (41%)
  starting transfers between devices  14.9 us (39%)
  Pallas kernels  6.34 us (17%)
  local copies, waits for them, and re-layouts  0.79 us (2%)
    ppermute x11, waiting for transfers between devices, exchange(): lax.ppermute(array, 'seq', [(i, i ^ mask) for i in range(lax.axis_size('s...  15.6 us
    ppermute x11, starting transfers between devices, exchange(): lax.ppermute(array, 'seq', [(i, i ^ mask) for i in range(lax.axis_size('s...  14.9 us
    pallas_call x9, Pallas kernels, call(): pl.pallas_call(kernel, out_shape=out_shape, in_specs=[VMEM_SPEC] * len(op...  6.34 us
    unnamed x8, local copies, waits for them, and re-layouts  0.79 us
  transfers between devices with their start and end apart: 11, of which 10 were waited for; matrix products, arithmetic and copies ran while one was open for 0% of the time, Pallas kernels for 6%

profile of v1, /device:TPU:0, one launch (start us, length us, event | category | flops | bytes accessed | tf_op | source)
XLA Modules:
  0.0 37.7 jit_solution(4812936776793072190)
XLA Ops:
  0.0 4.1 %collective-permute-start = (bf16[4,5120]{1,0:T(4,128)(2,1)}, bf16[4,5120]{1,0:T(4,128)(2,1)S(1)}, u32[]{:S(2)}, u32[]{:S(2)}) collective-permute-start(bf16[4,5120]{1,0:T(4,128)(2,1)} %refs_0_.1), channel_id=1, source_target_pairs={{0,8},{1,9},{2,10},{3,11},{4,12},{5,13},{6,14},{7,15},{8,0},{9,1},... | collective-permute-start | bytes 122888 | tf_op jit(solution)/shard_map/ppermute | solution.py:213
  4.1 2.6 %collective-permute-done.refs_1_ = bf16[4,5120]{1,0:T(4,128)(2,1)S(1)} collective-permute-done((bf16[4,5120]{1,0:T(4,128)(2,1)}, bf16[4,5120]{1,0:T(4,128)(2,1)S(1)}, u32[]{:S(2)}, u32[]{:S(2)}) %collective-permute-start) | collective-permute-done | bytes 40992 | tf_op jit(solution)/shard_map/ppermute | solution.py:213
  6.7 0.8 %copy-done.2 = bf16[4,5120]{1,0:T(4,128)(2,1)S(1)} copy-done((bf16[4,5120]{1,0:T(4,128)(2,1)S(1)}, bf16[4,5120]{1,0:T(4,128)(2,1)}, u32[]{:S(2)}) %copy-start.2) | copy-done | bytes 40984
  7.5 2.5 %collective-permute-start.1 = (bf16[8,5120]{1,0:T(8,128)(2,1)S(1)}, bf16[8,5120]{1,0:T(8,128)(2,1)S(1)}, u32[]{:S(2)}, u32[]{:S(2)}) collective-permute-start(bf16[8,5120]{1,0:T(8,128)(2,1)S(1)} %shard_map.46.refs_0_), channel_id=1, source_target_pairs={{0,6},{1,7},{2,4},{3,5},{4,2},{5,3},{6,0},{7,1},{8,14},{9,15},{10,... | collective-permute-start | bytes 245768 | tf_op jit(solution)/shard_map/ppermute | solution.py:213
  10.0 0.5 %collective-permute-start.2 = (bf16[8,5120]{1,0:T(8,128)(2,1)S(1)}, bf16[8,5120]{1,0:T(8,128)(2,1)S(1)}, u32[]{:S(2)}, u32[]{:S(2)}) collective-permute-start(bf16[8,5120]{1,0:T(8,128)(2,1)S(1)} %shard_map.46.refs_0_), channel_id=1, source_target_pairs={{0,2},{1,3},{2,0},{3,1},{4,6},{5,7},{6,4},{7,5},{8,10},{9,11},{10,... | collective-permute-start | bytes 245768 | tf_op jit(solution)/shard_map/ppermute | solution.py:213
  10.5 0.6 %collective-permute-start.3 = (bf16[8,5120]{1,0:T(8,128)(2,1)S(1)}, bf16[8,5120]{1,0:T(8,128)(2,1)S(1)}, u32[]{:S(2)}, u32[]{:S(2)}) collective-permute-start(bf16[8,5120]{1,0:T(8,128)(2,1)S(1)} %shard_map.46.refs_0_), channel_id=1, source_target_pairs={{0,4},{1,5},{2,6},{3,7},{4,0},{5,1},{6,2},{7,3},{8,12},{9,13},{10,... | collective-permute-start | bytes 245768 | tf_op jit(solution)/shard_map/ppermute | solution.py:213
  11.1 2.5 %collective-permute-done.1.refs_1_ = bf16[8,5120]{1,0:T(8,128)(2,1)S(1)} collective-permute-done((bf16[8,5120]{1,0:T(8,128)(2,1)S(1)}, bf16[8,5120]{1,0:T(8,128)(2,1)S(1)}, u32[]{:S(2)}, u32[]{:S(2)}) %collective-permute-start.1) | collective-permute-done | bytes 81952 | tf_op jit(solution)/shard_map/ppermute | solution.py:213
  13.6 0.9 %collective-permute-done.2.refs_2_ = bf16[8,5120]{1,0:T(8,128)(2,1)S(1)} collective-permute-done((bf16[8,5120]{1,0:T(8,128)(2,1)S(1)}, bf16[8,5120]{1,0:T(8,128)(2,1)S(1)}, u32[]{:S(2)}, u32[]{:S(2)}) %collective-permute-start.2) | collective-permute-done | bytes 81952 | tf_op jit(solution)/shard_map/ppermute | solution.py:213
  14.5 0.5 %collective-permute-done.3.refs_3_ = bf16[8,5120]{1,0:T(8,128)(2,1)S(1)} collective-permute-done((bf16[8,5120]{1,0:T(8,128)(2,1)S(1)}, bf16[8,5120]{1,0:T(8,128)(2,1)S(1)}, u32[]{:S(2)}, u32[]{:S(2)}) %collective-permute-start.3) | collective-permute-done | bytes 81952 | tf_op jit(solution)/shard_map/ppermute | solution.py:213
  15.1 1.6 %collective-permute-done.4.query_there_ref = bf16[32,5120]{1,0:T(8,128)(2,1)S(1)} collective-permute-done((bf16[32,5120]{1,0:T(8,128)(2,1)S(1)}, bf16[32,5120]{1,0:T(8,128)(2,1)S(1)}, u32[]{:S(2)}, u32[]{:S(2)}) %collective-permute-start.4) | collective-permute-done | bytes 327712 | tf_op jit(solution)/shard_map/ppermute | solution.py:213
  16.7 1.9 %shard_map.49 = (f32[32,2816]{1,0:T(8,128)S(1)}, f32[32,2816]{1,0:T(8,128)S(1)}) custom-call(bf16[32,5120]{1,0:T(8,128)(2,1)S(1)} %shard_map.47.query_here_ref, bf16[32,5120]{1,0:T(8,128)(2,1)S(1)} %collective-permute-done.4.query_there_ref, bf16[512,5120]{1,0:T(8,128)(2,1)S(1)} %copy-done, bf16[512,5120]{1,0:T(8,128)(2,1)S(1)} %copy-done.1), custom_call_target="tpu_custom_call" | custom-call | flops 335544320 | bytes 11862016 | tf_op jit(solution)/shard_map/pallas_call | solution.py:200
  18.9 1.9 %shard_map.48 = (f32[32,2816]{1,0:T(8,128)S(1)}, f32[32,2816]{1,0:T(8,128)S(1)}) custom-call(bf16[32,5120]{1,0:T(8,128)(2,1)S(1)} %shard_map.47.query_here_ref, bf16[32,5120]{1,0:T(8,128)(2,1)S(1)} %collective-permute-done.4.query_there_ref, bf16[512,5120]{1,0:T(8,128)(2,1)S(1)} %copy-done, bf16[512,5120]{1,0:T(8,128)(2,1)S(1)} %copy-done.1), custom_call_target="tpu_custom_call" | custom-call | flops 335544320 | bytes 11862016 | tf_op jit(solution)/shard_map/pallas_call | solution.py:200
  20.8 0.4 %collective-permute-start.5 = (f32[32,2816]{1,0:T(8,128)S(1)}, f32[32,2816]{1,0:T(8,128)S(1)}, u32[]{:S(2)}, u32[]{:S(2)}) collective-permute-start(f32[32,2816]{1,0:T(8,128)S(1)} %get-tuple-element.20), channel_id=1, source_target_pairs={{0,1},{1,0},{2,3},{3,2},{4,5},{5,4},{6,7},{7,6},{8,9},{9,8},{10,11... | collective-permute-start | bytes 1081352 | tf_op jit(solution)/shard_map/ppermute | solution.py:213
  21.2 0.4 %shard_map.50 = (f32[8,5632]{1,0:T(8,128)S(1)}, bf16[8,5376]{1,0:T(8,128)(2,1)S(1)}, bf16[8,5376]{1,0:T(8,128)(2,1)S(1)}, bf16[8,5376]{1,0:T(8,128)(2,1)S(1)}) custom-call(f32[32,2816]{1,0:T(8,128)S(1)} %get-tuple-element.21.refs_0_, f32[32,2816]{1,0:T(8,128)S(1)} %collective-permute-done.6.refs_1_), custom_call_target="tpu_custom_call" | custom-call | bytes 1159168 | tf_op jit(solution)/shard_map/pallas_call | solution.py:200
  21.6 0.9 %collective-permute-done.5.refs_1_ = f32[32,2816]{1,0:T(8,128)S(1)} collective-permute-done((f32[32,2816]{1,0:T(8,128)S(1)}, f32[32,2816]{1,0:T(8,128)S(1)}, u32[]{:S(2)}, u32[]{:S(2)}) %collective-permute-start.5) | collective-permute-done | bytes 360480 | tf_op jit(solution)/shard_map/ppermute | solution.py:213
  22.5 0.4 %shard_map.51 = (f32[8,5632]{1,0:T(8,128)S(1)}, bf16[8,5376]{1,0:T(8,128)(2,1)S(1)}, bf16[8,5376]{1,0:T(8,128)(2,1)S(1)}, bf16[8,5376]{1,0:T(8,128)(2,1)S(1)}) custom-call(f32[32,2816]{1,0:T(8,128)S(1)} %get-tuple-element.19.refs_0_, ...), custom_call_target="tpu_custom_call", output_to_operand_aliasing={{0}: (2, {}), {1}: (3, {}), {2}: (4, {}), {3}: (5, {})} | custom-call | bytes 1597440 | tf_op jit(solution)/shard_map/pallas_call | solution.py:200
  22.9 1.8 %collective-permute-start.7 = (bf16[8,5376]{1,0:T(8,128)(2,1)S(1)}, bf16[8,5376]{1,0:T(8,128)(2,1)S(1)}, u32[]{:S(2)}, u32[]{:S(2)}) collective-permute-start(bf16[8,5376]{1,0:T(8,128)(2,1)S(1)} %get-tuple-element.28), channel_id=1, source_target_pairs={{0,6},{1,7},{2,4},{3,5},{4,2},{5,3},{6,0},{7,1},{8,14},{9,15},{10,... | collective-permute-start | bytes 258056 | tf_op jit(solution)/shard_map/ppermute | solution.py:213
  25.0 1.5 %collective-permute-start.9 = (bf16[8,5376]{1,0:T(8,128)(2,1)S(1)}, bf16[8,5376]{1,0:T(8,128)(2,1)S(1)}, u32[]{:S(2)}, u32[]{:S(2)}) collective-permute-start(bf16[8,5376]{1,0:T(8,128)(2,1)S(1)} %get-tuple-element.30), channel_id=1, source_target_pairs={{0,4},{1,5},{2,6},{3,7},{4,0},{5,1},{6,2},{7,3},{8,12},{9,13},{10,... | collective-permute-start | bytes 258056 | tf_op jit(solution)/shard_map/ppermute | solution.py:213
  26.5 2.3 %collective-permute-done.7.refs_1_ = bf16[8,5376]{1,0:T(8,128)(2,1)S(1)} collective-permute-done((bf16[8,5376]{1,0:T(8,128)(2,1)S(1)}, bf16[8,5376]{1,0:T(8,128)(2,1)S(1)}, u32[]{:S(2)}, u32[]{:S(2)}) %collective-permute-start.7) | collective-permute-done | bytes 86048 | tf_op jit(solution)/shard_map/ppermute | solution.py:213
  28.8 1.7 %collective-permute-done.8.refs_2_ = bf16[8,5376]{1,0:T(8,128)(2,1)S(1)} collective-permute-done((bf16[8,5376]{1,0:T(8,128)(2,1)S(1)}, bf16[8,5376]{1,0:T(8,128)(2,1)S(1)}, u32[]{:S(2)}, u32[]{:S(2)}) %collective-permute-start.8) | collective-permute-done | bytes 86048 | tf_op jit(solution)/shard_map/ppermute | solution.py:213
  30.7 0.5 %shard_map.52 = (f32[4,5632]{1,0:T(4,128)S(1)}, bf16[4,5376]{1,0:T(4,128)(2,1)S(1)}) custom-call(f32[8,5632]{1,0:T(8,128)S(1)} %get-tuple-element.27.refs_0_, bf16[8,5376]{1,0:T(8,128)(2,1)S(1)} %collective-permute-done.7.refs_1_, bf16[8,5376]{1,0:T(8,128)(2,1)S(1)} %collective-permute-done.8.refs_2_, bf16[8,5376]{1,0:T(8,128)(2,1)S(1)} %collective-permute-done.9.refs_3_), custom_call_target="tpu_custom_call" | custom-call | bytes 571392 | tf_op jit(solution)/shard_map/pallas_call | solution.py:200
  31.2 3.0 %collective-permute-start.10 = (bf16[4,5376]{1,0:T(4,128)(2,1)S(1)}, bf16[4,5376]{1,0:T(4,128)(2,1)S(1)}, u32[]{:S(2)}, u32[]{:S(2)}) collective-permute-start(bf16[4,5376]{1,0:T(4,128)(2,1)S(1)} %get-tuple-element.32), channel_id=1, source_target_pairs={{0,8},{1,9},{2,10},{3,11},{4,12},{5,13},{6,14},{7,15},{8,0},{9,1},... | collective-permute-start | bytes 129032 | tf_op jit(solution)/shard_map/ppermute | solution.py:213
  34.2 2.5 %collective-permute-done.10.refs_1_ = bf16[4,5376]{1,0:T(4,128)(2,1)S(1)} collective-permute-done((bf16[4,5376]{1,0:T(4,128)(2,1)S(1)}, bf16[4,5376]{1,0:T(4,128)(2,1)S(1)}, u32[]{:S(2)}, u32[]{:S(2)}) %collective-permute-start.10) | collective-permute-done | bytes 43040 | tf_op jit(solution)/shard_map/ppermute | solution.py:213
  36.7 1.0 %shard_map.54 = bf16[4,5120]{1,0:T(4,128)(2,1)} custom-call(f32[4,5632]{1,0:T(4,128)S(1)} %get-tuple-element.31.refs_0_, bf16[4,5376]{1,0:T(4,128)(2,1)S(1)} %collective-permute-done.10.refs_1_, f32[1,5120]{1,0:T(1,128)S(1)} %shard_map.53.refs_2_), custom_call_target="tpu_custom_call" | custom-call | bytes 194560 | tf_op jit(solution)/shard_map/pallas_call | solution.py:200
  (15 shorter events, 0.8 us)
Async XLA Ops:
  0.0 16.7 %copy-start = (bf16[512,5120]{1,0:T(8,128)(2,1)S(1)}, bf16[512,5120]{1,0:T(8,128)(2,1)}, u32[]{:S(2)}) copy-start(bf16[512,5120]{1,0:T(8,128)(2,1)} %key_ref.3) | copy-start | bytes 15728644
  0.0 16.7 %copy-start.1 = (bf16[512,5120]{1,0:T(8,128)(2,1)S(1)}, bf16[512,5120]{1,0:T(8,128)(2,1)}, u32[]{:S(2)}) copy-start(bf16[512,5120]{1,0:T(8,128)(2,1)} %value_ref.3) | copy-start | bytes 15728644
  0.0 6.7 %collective-permute-start = (bf16[4,5120]{1,0:T(4,128)(2,1)}, bf16[4,5120]{1,0:T(4,128)(2,1)S(1)}, u32[]{:S(2)}, u32[]{:S(2)}) collective-permute-start(bf16[4,5120]{1,0:T(4,128)(2,1)} %refs_0_.1), channel_id=1, source_target_pairs={{0,8},{1,9},{2,10},{3,11},{4,12},{5,13},{6,14},{7,15},{8,0},{9,1},... | collective-permute-start | bytes 122888 | tf_op jit(solution)/shard_map/ppermute | solution.py:213
  6.7 0.8 %copy-start.2 = (bf16[4,5120]{1,0:T(4,128)(2,1)S(1)}, bf16[4,5120]{1,0:T(4,128)(2,1)}, u32[]{:S(2)}) copy-start(bf16[4,5120]{1,0:T(4,128)(2,1)} %refs_0_.1) | copy-start | bytes 122884
  7.5 6.1 %collective-permute-start.1 = (bf16[8,5120]{1,0:T(8,128)(2,1)S(1)}, bf16[8,5120]{1,0:T(8,128)(2,1)S(1)}, u32[]{:S(2)}, u32[]{:S(2)}) collective-permute-start(bf16[8,5120]{1,0:T(8,128)(2,1)S(1)} %shard_map.46.refs_0_), channel_id=1, source_target_pairs={{0,6},{1,7},{2,4},{3,5},{4,2},{5,3},{6,0},{7,1},{8,14},{9,15},{10,... | collective-permute-start | bytes 245768 | tf_op jit(solution)/shard_map/ppermute | solution.py:213
  10.0 4.5 %collective-permute-start.2 = (bf16[8,5120]{1,0:T(8,128)(2,1)S(1)}, bf16[8,5120]{1,0:T(8,128)(2,1)S(1)}, u32[]{:S(2)}, u32[]{:S(2)}) collective-permute-start(bf16[8,5120]{1,0:T(8,128)(2,1)S(1)} %shard_map.46.refs_0_), channel_id=1, source_target_pairs={{0,2},{1,3},{2,0},{3,1},{4,6},{5,7},{6,4},{7,5},{8,10},{9,11},{10,... | collective-permute-start | bytes 245768 | tf_op jit(solution)/shard_map/ppermute | solution.py:213
  10.5 4.4 %collective-permute-start.3 = (bf16[8,5120]{1,0:T(8,128)(2,1)S(1)}, bf16[8,5120]{1,0:T(8,128)(2,1)S(1)}, u32[]{:S(2)}, u32[]{:S(2)}) collective-permute-start(bf16[8,5120]{1,0:T(8,128)(2,1)S(1)} %shard_map.46.refs_0_), channel_id=1, source_target_pairs={{0,4},{1,5},{2,6},{3,7},{4,0},{5,1},{6,2},{7,3},{8,12},{9,13},{10,... | collective-permute-start | bytes 245768 | tf_op jit(solution)/shard_map/ppermute | solution.py:213
  15.0 1.7 %collective-permute-start.4 = (bf16[32,5120]{1,0:T(8,128)(2,1)S(1)}, bf16[32,5120]{1,0:T(8,128)(2,1)S(1)}, u32[]{:S(2)}, u32[]{:S(2)}) collective-permute-start(bf16[32,5120]{1,0:T(8,128)(2,1)S(1)} %shard_map.47.query_here_ref), channel_id=1, source_target_pairs={{0,1},{1,0},{2,3},{3,2},{4,5},{5,4},{6,7},{7,6},{8,9},{9,8},{10,11... | collective-permute-start | bytes 983048 | tf_op jit(solution)/shard_map/ppermute | solution.py:213
  18.6 15.6 %copy-start.3 = (f32[5120]{0:T(1024)S(1)}, f32[5120]{0:T(1024)}, u32[]{:S(2)}) copy-start(f32[5120]{0:T(1024)} %param.7) | copy-start | bytes 61444
  18.6 2.6 %collective-permute-start.6 = (f32[32,2816]{1,0:T(8,128)S(1)}, f32[32,2816]{1,0:T(8,128)S(1)}, u32[]{:S(2)}, u32[]{:S(2)}) collective-permute-start(f32[32,2816]{1,0:T(8,128)S(1)} %get-tuple-element.22), channel_id=1, source_target_pairs={{0,1},{1,0},{2,3},{3,2},{4,5},{5,4},{6,7},{7,6},{8,9},{9,8},{10,11... | collective-permute-start | bytes 1081352 | tf_op jit(solution)/shard_map/ppermute | solution.py:213
  20.8 1.7 %collective-permute-start.5 = (f32[32,2816]{1,0:T(8,128)S(1)}, f32[32,2816]{1,0:T(8,128)S(1)}, u32[]{:S(2)}, u32[]{:S(2)}) collective-permute-start(f32[32,2816]{1,0:T(8,128)S(1)} %get-tuple-element.20), channel_id=1, source_target_pairs={{0,1},{1,0},{2,3},{3,2},{4,5},{5,4},{6,7},{7,6},{8,9},{9,8},{10,11... | collective-permute-start | bytes 1081352 | tf_op jit(solution)/shard_map/ppermute | solution.py:213
  22.9 5.9 %collective-permute-start.7 = (bf16[8,5376]{1,0:T(8,128)(2,1)S(1)}, bf16[8,5376]{1,0:T(8,128)(2,1)S(1)}, u32[]{:S(2)}, u32[]{:S(2)}) collective-permute-start(bf16[8,5376]{1,0:T(8,128)(2,1)S(1)} %get-tuple-element.28), channel_id=1, source_target_pairs={{0,6},{1,7},{2,4},{3,5},{4,2},{5,3},{6,0},{7,1},{8,14},{9,15},{10,... | collective-permute-start | bytes 258056 | tf_op jit(solution)/shard_map/ppermute | solution.py:213
  24.7 5.8 %collective-permute-start.8 = (bf16[8,5376]{1,0:T(8,128)(2,1)S(1)}, bf16[8,5376]{1,0:T(8,128)(2,1)S(1)}, u32[]{:S(2)}, u32[]{:S(2)}) collective-permute-start(bf16[8,5376]{1,0:T(8,128)(2,1)S(1)} %get-tuple-element.29), channel_id=1, source_target_pairs={{0,2},{1,3},{2,0},{3,1},{4,6},{5,7},{6,4},{7,5},{8,10},{9,11},{10,... | collective-permute-start | bytes 258056 | tf_op jit(solution)/shard_map/ppermute | solution.py:213
  25.0 5.6 %collective-permute-start.9 = (bf16[8,5376]{1,0:T(8,128)(2,1)S(1)}, bf16[8,5376]{1,0:T(8,128)(2,1)S(1)}, u32[]{:S(2)}, u32[]{:S(2)}) collective-permute-start(bf16[8,5376]{1,0:T(8,128)(2,1)S(1)} %get-tuple-element.30), channel_id=1, source_target_pairs={{0,4},{1,5},{2,6},{3,7},{4,0},{5,1},{6,2},{7,3},{8,12},{9,13},{10,... | collective-permute-start | bytes 258056 | tf_op jit(solution)/shard_map/ppermute | solution.py:213
  31.2 5.4 %collective-permute-start.10 = (bf16[4,5376]{1,0:T(4,128)(2,1)S(1)}, bf16[4,5376]{1,0:T(4,128)(2,1)S(1)}, u32[]{:S(2)}, u32[]{:S(2)}) collective-permute-start(bf16[4,5376]{1,0:T(4,128)(2,1)S(1)} %get-tuple-element.32), channel_id=1, source_target_pairs={{0,8},{1,9},{2,10},{3,11},{4,12},{5,13},{6,14},{7,15},{8,0},{9,1},... | collective-permute-start | bytes 129032 | tf_op jit(solution)/shard_map/ppermute | solution.py:213

commit v2 on v1

--- a/solution.py
+++ b/solution.py
@@ -20,8 +20,12 @@
     out_ref[...] = source_ref[...]
 
 
-def join_kernel(*refs):
-    refs[-1][...] = jnp.concatenate([ref[...] for ref in refs[:-1]], axis=0)
+def join_kernel(*refs, count):
+    first = 0
+    for out_ref in refs[count:]:
+        columns = slice(first, first + out_ref.shape[1])
+        out_ref[...] = jnp.concatenate([ref[:, columns] for ref in refs[:count]], axis=0)
+        first = columns.stop
 
 
 def attend_kernel(
@@ -36,10 +40,10 @@
         return slice((first_head + head) * HDIM, (first_head + head + 1) * HDIM)
 
     def score(head):
-        columns = shifted(head)
+        columns = slice(head * HDIM, (head + 1) * HDIM)
         dots_ref[head % slots] = lax.dot_general(
             jnp.concatenate([query_here_ref[:, columns], query_there_ref[:, columns]], axis=0),
-            key_ref[:, columns],
+            key_ref[:, shifted(head)],
             (((1,), (1,)), ((), ())),
             preferred_element_type=jnp.float32,
         )
@@ -227,13 +231,14 @@
     tokens = keys.shape[0]
     gain = call(copy_kernel, jax.ShapeDtypeStruct((1, width), gain.dtype), [gain.reshape(1, width)], FETCH_FLOPS)
 
-    window = queries
+    windows = [queries]
     for masks in reversed(stages):
-        pieces = [window, *(exchange(window, mask) for mask in masks)]
-        shape = jax.ShapeDtypeStruct((len(pieces) * window.shape[0], width), window.dtype)
-        window = call(join_kernel, shape, pieces, FETCH_FLOPS)
-    arrived = exchange(window, core)
-    count = window.shape[0]
+        pieces = [windows[0], *(exchange(windows[0], mask) for mask in masks)]
+        parts = CHAINS if masks is stages[0] else 1
+        shape = jax.ShapeDtypeStruct((len(pieces) * windows[0].shape[0], width // parts), queries.dtype)
+        kernel = functools.partial(join_kernel, count=len(pieces))
+        windows = call(kernel, (shape,) * parts, pieces, FETCH_FLOPS)
+    count = windows[0].shape[0]
 
     plain = lambda count, parts: jax.ShapeDtypeStruct((count, parts * (part + 2 * HDIM)), jnp.float32)
     code = lambda count: jax.ShapeDtypeStruct((count, CHAINS * (part + HDIM)), jnp.bfloat16)
@@ -254,7 +259,7 @@
         keep, send = call(
             functools.partial(attend_kernel, first_head=chain * part // HDIM),
             (plain(count, 1), plain(count, 1)),
-            (window, arrived, keys, values),
+            (windows[chain], exchange(windows[chain], core), keys, values),
             8 * count * tokens * part,
             [pltpu.VMEM((4, 2 * count, tokens), jnp.float32), pltpu.VMEM((4, 4 * count, tokens), jnp.bfloat16)],
             16 << 20,

time: 37.9 us -> 39 us (1.029)
  waiting for transfers between devices: 15.6 us -> 16.2 us
  starting transfers between devices: 14.9 us -> 15.4 us
    ppermute x11 -> x12, waiting for transfers between devices: 15.6 us -> 16.2 us  [exchange(): lax.ppermute(array, 'seq', [(i, i ^ mask) for i in range(lax.axis_size('s...]
    ppermute x11 -> x12, starting transfers between devices: 14.9 us -> 15.4 us  [exchange(): lax.ppermute(array, 'seq', [(i, i ^ mask) for i in range(lax.axis_size('s...]
  transfers between devices with their start and end apart: 11 -> 12, of which waited for: 10 -> 10; matrix products, arithmetic and copies ran while one was open for 0% -> 0% of each run, Pallas kernels for 6% -> 11%
where the time goes in v2:
time: 39 us; the launch traced here: 38.8 us
  waiting for transfers between devices  16.2 us (42%)
  starting transfers between devices  15.4 us (39%)
  Pallas kernels  6.4 us (16%)
  local copies, waits for them, and re-layouts  0.79 us (2%)
    ppermute x12, waiting for transfers between devices, exchange(): lax.ppermute(array, 'seq', [(i, i ^ mask) for i in range(lax.axis_size('s...  16.2 us
    ppermute x12, starting transfers between devices, exchange(): lax.ppermute(array, 'seq', [(i, i ^ mask) for i in range(lax.axis_size('s...  15.4 us
    pallas_call x9, Pallas kernels, call(): pl.pallas_call(kernel, out_shape=out_shape, in_specs=[VMEM_SPEC] * len(op...  6.4 us
    unnamed x8, local copies, waits for them, and re-layouts  0.79 us
  transfers between devices with their start and end apart: 12, of which 10 were waited for; matrix products, arithmetic and copies ran while one was open for 0% of the time, Pallas kernels for 11%

profile of v2, /device:TPU:0, one launch (start us, length us, event | category | flops | bytes accessed | tf_op | source)
XLA Modules:
  0.0 38.8 jit_solution(10497907091148469237)
XLA Ops:
  0.0 4.1 %collective-permute-start = (bf16[4,5120]{1,0:T(4,128)(2,1)}, bf16[4,5120]{1,0:T(4,128)(2,1)S(1)}, u32[]{:S(2)}, u32[]{:S(2)}) collective-permute-start(bf16[4,5120]{1,0:T(4,128)(2,1)} %refs_0_.1), channel_id=1, source_target_pairs={{0,8},{1,9},{2,10},{3,11},{4,12},{5,13},{6,14},{7,15},{8,0},{9,1},... | collective-permute-start | bytes 122888 | tf_op jit(solution)/shard_map/ppermute | solution.py:217
  4.1 2.6 %collective-permute-done.refs_1_ = bf16[4,5120]{1,0:T(4,128)(2,1)S(1)} collective-permute-done((bf16[4,5120]{1,0:T(4,128)(2,1)}, bf16[4,5120]{1,0:T(4,128)(2,1)S(1)}, u32[]{:S(2)}, u32[]{:S(2)}) %collective-permute-start) | collective-permute-done | bytes 40992 | tf_op jit(solution)/shard_map/ppermute | solution.py:217
  6.7 0.8 %copy-done.2 = bf16[4,5120]{1,0:T(4,128)(2,1)S(1)} copy-done((bf16[4,5120]{1,0:T(4,128)(2,1)S(1)}, bf16[4,5120]{1,0:T(4,128)(2,1)}, u32[]{:S(2)}) %copy-start.2) | copy-done | bytes 40984
  7.5 2.5 %collective-permute-start.1 = (bf16[8,5120]{1,0:T(8,128)(2,1)S(1)}, bf16[8,5120]{1,0:T(8,128)(2,1)S(1)}, u32[]{:S(2)}, u32[]{:S(2)}) collective-permute-start(bf16[8,5120]{1,0:T(8,128)(2,1)S(1)} %shard_map.46.refs_0_), channel_id=1, source_target_pairs={{0,6},{1,7},{2,4},{3,5},{4,2},{5,3},{6,0},{7,1},{8,14},{9,15},{10,... | collective-permute-start | bytes 245768 | tf_op jit(solution)/shard_map/ppermute | solution.py:217
  10.0 0.5 %collective-permute-start.2 = (bf16[8,5120]{1,0:T(8,128)(2,1)S(1)}, bf16[8,5120]{1,0:T(8,128)(2,1)S(1)}, u32[]{:S(2)}, u32[]{:S(2)}) collective-permute-start(bf16[8,5120]{1,0:T(8,128)(2,1)S(1)} %shard_map.46.refs_0_), channel_id=1, source_target_pairs={{0,2},{1,3},{2,0},{3,1},{4,6},{5,7},{6,4},{7,5},{8,10},{9,11},{10,... | collective-permute-start | bytes 245768 | tf_op jit(solution)/shard_map/ppermute | solution.py:217
  10.5 0.6 %collective-permute-start.3 = (bf16[8,5120]{1,0:T(8,128)(2,1)S(1)}, bf16[8,5120]{1,0:T(8,128)(2,1)S(1)}, u32[]{:S(2)}, u32[]{:S(2)}) collective-permute-start(bf16[8,5120]{1,0:T(8,128)(2,1)S(1)} %shard_map.46.refs_0_), channel_id=1, source_target_pairs={{0,4},{1,5},{2,6},{3,7},{4,0},{5,1},{6,2},{7,3},{8,12},{9,13},{10,... | collective-permute-start | bytes 245768 | tf_op jit(solution)/shard_map/ppermute | solution.py:217
  11.1 2.5 %collective-permute-done.1.refs_1_ = bf16[8,5120]{1,0:T(8,128)(2,1)S(1)} collective-permute-done((bf16[8,5120]{1,0:T(8,128)(2,1)S(1)}, bf16[8,5120]{1,0:T(8,128)(2,1)S(1)}, u32[]{:S(2)}, u32[]{:S(2)}) %collective-permute-start.1) | collective-permute-done | bytes 81952 | tf_op jit(solution)/shard_map/ppermute | solution.py:217
  13.6 0.9 %collective-permute-done.2.refs_2_ = bf16[8,5120]{1,0:T(8,128)(2,1)S(1)} collective-permute-done((bf16[8,5120]{1,0:T(8,128)(2,1)S(1)}, bf16[8,5120]{1,0:T(8,128)(2,1)S(1)}, u32[]{:S(2)}, u32[]{:S(2)}) %collective-permute-start.2) | collective-permute-done | bytes 81952 | tf_op jit(solution)/shard_map/ppermute | solution.py:217
  14.5 0.5 %collective-permute-done.3.refs_3_ = bf16[8,5120]{1,0:T(8,128)(2,1)S(1)} collective-permute-done((bf16[8,5120]{1,0:T(8,128)(2,1)S(1)}, bf16[8,5120]{1,0:T(8,128)(2,1)S(1)}, u32[]{:S(2)}, u32[]{:S(2)}) %collective-permute-start.3) | collective-permute-done | bytes 81952 | tf_op jit(solution)/shard_map/ppermute | solution.py:217
  15.1 0.5 %collective-permute-start.4 = (bf16[32,2560]{1,0:T(8,128)(2,1)S(1)}, bf16[32,2560]{1,0:T(8,128)(2,1)S(1)}, u32[]{:S(2)}, u32[]{:S(2)}) collective-permute-start(bf16[32,2560]{1,0:T(8,128)(2,1)S(1)} %get-tuple-element.21.query_here_ref), channel_id=1, source_target_pairs={{0,1},{1,0},{2,3},{3,2},{4,5},{5,4},{6,7},{7,6},{8,9},{9,8},{10,11... | collective-permute-start | bytes 491528 | tf_op jit(solution)/shard_map/ppermute | solution.py:217
  15.6 0.9 %collective-permute-done.6.query_there_ref = bf16[32,2560]{1,0:T(8,128)(2,1)S(1)} collective-permute-done((bf16[32,2560]{1,0:T(8,128)(2,1)S(1)}, bf16[32,2560]{1,0:T(8,128)(2,1)S(1)}, u32[]{:S(2)}, u32[]{:S(2)}) %collective-permute-start.6) | collective-permute-done | bytes 163872 | tf_op jit(solution)/shard_map/ppermute | solution.py:217
  16.5 1.9 %shard_map.49 = (f32[32,2816]{1,0:T(8,128)S(1)}, f32[32,2816]{1,0:T(8,128)S(1)}) custom-call(bf16[32,2560]{1,0:T(8,128)(2,1)S(1)} %get-tuple-element.24.query_here_ref, bf16[32,2560]{1,0:T(8,128)(2,1)S(1)} %collective-permute-done.6.query_there_ref, bf16[512,5120]{1,0:T(8,128)(2,1)S(1)} %copy-done, bf16[512,5120]{1,0:T(8,128)(2,1)S(1)} %copy-done.1), custom_call_target="tpu_custom_call" | custom-call | flops 335544320 | bytes 11534336 | tf_op jit(solution)/shard_map/pallas_call | solution.py:204
  18.6 1.9 %shard_map.48 = (f32[32,2816]{1,0:T(8,128)S(1)}, f32[32,2816]{1,0:T(8,128)S(1)}) custom-call(bf16[32,2560]{1,0:T(8,128)(2,1)S(1)} %get-tuple-element.21.query_here_ref, bf16[32,2560]{1,0:T(8,128)(2,1)S(1)} %collective-permute-done.4.query_there_ref, bf16[512,5120]{1,0:T(8,128)(2,1)S(1)} %copy-done, bf16[512,5120]{1,0:T(8,128)(2,1)S(1)} %copy-done.1), custom_call_target="tpu_custom_call" | custom-call | flops 335544320 | bytes 11534336 | tf_op jit(solution)/shard_map/pallas_call | solution.py:204
  21.5 0.9 %collective-permute-done.5.refs_1_ = f32[32,2816]{1,0:T(8,128)S(1)} collective-permute-done((f32[32,2816]{1,0:T(8,128)S(1)}, f32[32,2816]{1,0:T(8,128)S(1)}, u32[]{:S(2)}, u32[]{:S(2)}) %collective-permute-start.5) | collective-permute-done | bytes 360480 | tf_op jit(solution)/shard_map/ppermute | solution.py:217
  22.8 0.6 %collective-permute-start.10 = (bf16[8,5376]{1,0:T(8,128)(2,1)S(1)}, bf16[8,5376]{1,0:T(8,128)(2,1)S(1)}, u32[]{:S(2)}, u32[]{:S(2)}) collective-permute-start(bf16[8,5376]{1,0:T(8,128)(2,1)S(1)} %get-tuple-element.34), channel_id=1, source_target_pairs={{0,4},{1,5},{2,6},{3,7},{4,0},{5,1},{6,2},{7,3},{8,12},{9,13},{10,... | collective-permute-start | bytes 258056 | tf_op jit(solution)/shard_map/ppermute | solution.py:217
  23.4 2.4 %collective-permute-start.8 = (bf16[8,5376]{1,0:T(8,128)(2,1)S(1)}, bf16[8,5376]{1,0:T(8,128)(2,1)S(1)}, u32[]{:S(2)}, u32[]{:S(2)}) collective-permute-start(bf16[8,5376]{1,0:T(8,128)(2,1)S(1)} %get-tuple-element.32), channel_id=1, source_target_pairs={{0,6},{1,7},{2,4},{3,5},{4,2},{5,3},{6,0},{7,1},{8,14},{9,15},{10,... | collective-permute-start | bytes 258056 | tf_op jit(solution)/shard_map/ppermute | solution.py:217
  25.8 0.5 %collective-permute-start.9 = (bf16[8,5376]{1,0:T(8,128)(2,1)S(1)}, bf16[8,5376]{1,0:T(8,128)(2,1)S(1)}, u32[]{:S(2)}, u32[]{:S(2)}) collective-permute-start(bf16[8,5376]{1,0:T(8,128)(2,1)S(1)} %get-tuple-element.33), channel_id=1, source_target_pairs={{0,2},{1,3},{2,0},{3,1},{4,6},{5,7},{6,4},{7,5},{8,10},{9,11},{10,... | collective-permute-start | bytes 258056 | tf_op jit(solution)/shard_map/ppermute | solution.py:217
  26.3 1.7 %collective-permute-done.10.refs_3_ = bf16[8,5376]{1,0:T(8,128)(2,1)S(1)} collective-permute-done((bf16[8,5376]{1,0:T(8,128)(2,1)S(1)}, bf16[8,5376]{1,0:T(8,128)(2,1)S(1)}, u32[]{:S(2)}, u32[]{:S(2)}) %collective-permute-start.10) | collective-permute-done | bytes 86048 | tf_op jit(solution)/shard_map/ppermute | solution.py:217
  28.0 2.5 %collective-permute-done.8.refs_1_ = bf16[8,5376]{1,0:T(8,128)(2,1)S(1)} collective-permute-done((bf16[8,5376]{1,0:T(8,128)(2,1)S(1)}, bf16[8,5376]{1,0:T(8,128)(2,1)S(1)}, u32[]{:S(2)}, u32[]{:S(2)}) %collective-permute-start.8) | collective-permute-done | bytes 86048 | tf_op jit(solution)/shard_map/ppermute | solution.py:217
  30.5 1.3 %collective-permute-done.9.refs_2_ = bf16[8,5376]{1,0:T(8,128)(2,1)S(1)} collective-permute-done((bf16[8,5376]{1,0:T(8,128)(2,1)S(1)}, bf16[8,5376]{1,0:T(8,128)(2,1)S(1)}, u32[]{:S(2)}, u32[]{:S(2)}) %collective-permute-start.9) | collective-permute-done | bytes 86048 | tf_op jit(solution)/shard_map/ppermute | solution.py:217
  31.8 0.5 %shard_map.52 = (f32[4,5632]{1,0:T(4,128)S(1)}, bf16[4,5376]{1,0:T(4,128)(2,1)S(1)}) custom-call(f32[8,5632]{1,0:T(8,128)S(1)} %get-tuple-element.31.refs_0_, bf16[8,5376]{1,0:T(8,128)(2,1)S(1)} %collective-permute-done.8.refs_1_, bf16[8,5376]{1,0:T(8,128)(2,1)S(1)} %collective-permute-done.9.refs_2_, bf16[8,5376]{1,0:T(8,128)(2,1)S(1)} %collective-permute-done.10.refs_3_), custom_call_target="tpu_custom_call" | custom-call | bytes 571392 | tf_op jit(solution)/shard_map/pallas_call | solution.py:204
  32.4 3.0 %collective-permute-start.11 = (bf16[4,5376]{1,0:T(4,128)(2,1)S(1)}, bf16[4,5376]{1,0:T(4,128)(2,1)S(1)}, u32[]{:S(2)}, u32[]{:S(2)}) collective-permute-start(bf16[4,5376]{1,0:T(4,128)(2,1)S(1)} %get-tuple-element.36), channel_id=1, source_target_pairs={{0,8},{1,9},{2,10},{3,11},{4,12},{5,13},{6,14},{7,15},{8,0},{9,1},... | collective-permute-start | bytes 129032 | tf_op jit(solution)/shard_map/ppermute | solution.py:217
  35.3 2.5 %collective-permute-done.11.refs_1_ = bf16[4,5376]{1,0:T(4,128)(2,1)S(1)} collective-permute-done((bf16[4,5376]{1,0:T(4,128)(2,1)S(1)}, bf16[4,5376]{1,0:T(4,128)(2,1)S(1)}, u32[]{:S(2)}, u32[]{:S(2)}) %collective-permute-start.11) | collective-permute-done | bytes 43040 | tf_op jit(solution)/shard_map/ppermute | solution.py:217
  37.8 1.0 %shard_map.54 = bf16[4,5120]{1,0:T(4,128)(2,1)} custom-call(f32[4,5632]{1,0:T(4,128)S(1)} %get-tuple-element.35.refs_0_, bf16[4,5376]{1,0:T(4,128)(2,1)S(1)} %collective-permute-done.11.refs_1_, f32[1,5120]{1,0:T(1,128)S(1)} %shard_map.53.refs_2_), custom_call_target="tpu_custom_call" | custom-call | bytes 194560 | tf_op jit(solution)/shard_map/pallas_call | solution.py:204
  (17 shorter events, 1.7 us)
Async XLA Ops:
  0.0 16.5 %copy-start = (bf16[512,5120]{1,0:T(8,128)(2,1)S(1)}, bf16[512,5120]{1,0:T(8,128)(2,1)}, u32[]{:S(2)}) copy-start(bf16[512,5120]{1,0:T(8,128)(2,1)} %key_ref.3) | copy-start | bytes 15728644
  0.0 16.5 %copy-start.1 = (bf16[512,5120]{1,0:T(8,128)(2,1)S(1)}, bf16[512,5120]{1,0:T(8,128)(2,1)}, u32[]{:S(2)}) copy-start(bf16[512,5120]{1,0:T(8,128)(2,1)} %value_ref.3) | copy-start | bytes 15728644
  0.0 6.7 %collective-permute-start = (bf16[4,5120]{1,0:T(4,128)(2,1)}, bf16[4,5120]{1,0:T(4,128)(2,1)S(1)}, u32[]{:S(2)}, u32[]{:S(2)}) collective-permute-start(bf16[4,5120]{1,0:T(4,128)(2,1)} %refs_0_.1), channel_id=1, source_target_pairs={{0,8},{1,9},{2,10},{3,11},{4,12},{5,13},{6,14},{7,15},{8,0},{9,1},... | collective-permute-start | bytes 122888 | tf_op jit(solution)/shard_map/ppermute | solution.py:217
  6.7 0.8 %copy-start.2 = (bf16[4,5120]{1,0:T(4,128)(2,1)S(1)}, bf16[4,5120]{1,0:T(4,128)(2,1)}, u32[]{:S(2)}) copy-start(bf16[4,5120]{1,0:T(4,128)(2,1)} %refs_0_.1) | copy-start | bytes 122884
  7.5 6.1 %collective-permute-start.1 = (bf16[8,5120]{1,0:T(8,128)(2,1)S(1)}, bf16[8,5120]{1,0:T(8,128)(2,1)S(1)}, u32[]{:S(2)}, u32[]{:S(2)}) collective-permute-start(bf16[8,5120]{1,0:T(8,128)(2,1)S(1)} %shard_map.46.refs_0_), channel_id=1, source_target_pairs={{0,6},{1,7},{2,4},{3,5},{4,2},{5,3},{6,0},{7,1},{8,14},{9,15},{10,... | collective-permute-start | bytes 245768 | tf_op jit(solution)/shard_map/ppermute | solution.py:217
  10.0 4.5 %collective-permute-start.2 = (bf16[8,5120]{1,0:T(8,128)(2,1)S(1)}, bf16[8,5120]{1,0:T(8,128)(2,1)S(1)}, u32[]{:S(2)}, u32[]{:S(2)}) collective-permute-start(bf16[8,5120]{1,0:T(8,128)(2,1)S(1)} %shard_map.46.refs_0_), channel_id=1, source_target_pairs={{0,2},{1,3},{2,0},{3,1},{4,6},{5,7},{6,4},{7,5},{8,10},{9,11},{10,... | collective-permute-start | bytes 245768 | tf_op jit(solution)/shard_map/ppermute | solution.py:217
  10.5 4.4 %collective-permute-start.3 = (bf16[8,5120]{1,0:T(8,128)(2,1)S(1)}, bf16[8,5120]{1,0:T(8,128)(2,1)S(1)}, u32[]{:S(2)}, u32[]{:S(2)}) collective-permute-start(bf16[8,5120]{1,0:T(8,128)(2,1)S(1)} %shard_map.46.refs_0_), channel_id=1, source_target_pairs={{0,4},{1,5},{2,6},{3,7},{4,0},{5,1},{6,2},{7,3},{8,12},{9,13},{10,... | collective-permute-start | bytes 245768 | tf_op jit(solution)/shard_map/ppermute | solution.py:217
  15.0 1.5 %collective-permute-start.6 = (bf16[32,2560]{1,0:T(8,128)(2,1)S(1)}, bf16[32,2560]{1,0:T(8,128)(2,1)S(1)}, u32[]{:S(2)}, u32[]{:S(2)}) collective-permute-start(bf16[32,2560]{1,0:T(8,128)(2,1)S(1)} %get-tuple-element.24.query_here_ref), channel_id=1, source_target_pairs={{0,1},{1,0},{2,3},{3,2},{4,5},{5,4},{6,7},{7,6},{8,9},{9,8},{10,11... | collective-permute-start | bytes 491528 | tf_op jit(solution)/shard_map/ppermute | solution.py:217
  15.1 3.6 %collective-permute-start.4 = (bf16[32,2560]{1,0:T(8,128)(2,1)S(1)}, bf16[32,2560]{1,0:T(8,128)(2,1)S(1)}, u32[]{:S(2)}, u32[]{:S(2)}) collective-permute-start(bf16[32,2560]{1,0:T(8,128)(2,1)S(1)} %get-tuple-element.21.query_here_ref), channel_id=1, source_target_pairs={{0,1},{1,0},{2,3},{3,2},{4,5},{5,4},{6,7},{7,6},{8,9},{9,8},{10,11... | collective-permute-start | bytes 491528 | tf_op jit(solution)/shard_map/ppermute | solution.py:217
  18.4 16.9 %copy-start.3 = (f32[5120]{0:T(1024)S(1)}, f32[5120]{0:T(1024)}, u32[]{:S(2)}) copy-start(f32[5120]{0:T(1024)} %param.7) | copy-start | bytes 61444
  18.4 2.6 %collective-permute-start.7 = (f32[32,2816]{1,0:T(8,128)S(1)}, f32[32,2816]{1,0:T(8,128)S(1)}, u32[]{:S(2)}, u32[]{:S(2)}) collective-permute-start(f32[32,2816]{1,0:T(8,128)S(1)} %get-tuple-element.26), channel_id=1, source_target_pairs={{0,1},{1,0},{2,3},{3,2},{4,5},{5,4},{6,7},{7,6},{8,9},{9,8},{10,11... | collective-permute-start | bytes 1081352 | tf_op jit(solution)/shard_map/ppermute | solution.py:217
  20.6 1.7 %collective-permute-start.5 = (f32[32,2816]{1,0:T(8,128)S(1)}, f32[32,2816]{1,0:T(8,128)S(1)}, u32[]{:S(2)}, u32[]{:S(2)}) collective-permute-start(f32[32,2816]{1,0:T(8,128)S(1)} %get-tuple-element.23), channel_id=1, source_target_pairs={{0,1},{1,0},{2,3},{3,2},{4,5},{5,4},{6,7},{7,6},{8,9},{9,8},{10,11... | collective-permute-start | bytes 1081352 | tf_op jit(solution)/shard_map/ppermute | solution.py:217
  22.8 5.3 %collective-permute-start.10 = (bf16[8,5376]{1,0:T(8,128)(2,1)S(1)}, bf16[8,5376]{1,0:T(8,128)(2,1)S(1)}, u32[]{:S(2)}, u32[]{:S(2)}) collective-permute-start(bf16[8,5376]{1,0:T(8,128)(2,1)S(1)} %get-tuple-element.34), channel_id=1, source_target_pairs={{0,4},{1,5},{2,6},{3,7},{4,0},{5,1},{6,2},{7,3},{8,12},{9,13},{10,... | collective-permute-start | bytes 258056 | tf_op jit(solution)/shard_map/ppermute | solution.py:217
  23.4 7.2 %collective-permute-start.8 = (bf16[8,5376]{1,0:T(8,128)(2,1)S(1)}, bf16[8,5376]{1,0:T(8,128)(2,1)S(1)}, u32[]{:S(2)}, u32[]{:S(2)}) collective-permute-start(bf16[8,5376]{1,0:T(8,128)(2,1)S(1)} %get-tuple-element.32), channel_id=1, source_target_pairs={{0,6},{1,7},{2,4},{3,5},{4,2},{5,3},{6,0},{7,1},{8,14},{9,15},{10,... | collective-permute-start | bytes 258056 | tf_op jit(solution)/shard_map/ppermute | solution.py:217
  25.8 6.0 %collective-permute-start.9 = (bf16[8,5376]{1,0:T(8,128)(2,1)S(1)}, bf16[8,5376]{1,0:T(8,128)(2,1)S(1)}, u32[]{:S(2)}, u32[]{:S(2)}) collective-permute-start(bf16[8,5376]{1,0:T(8,128)(2,1)S(1)} %get-tuple-element.33), channel_id=1, source_target_pairs={{0,2},{1,3},{2,0},{3,1},{4,6},{5,7},{6,4},{7,5},{8,10},{9,11},{10,... | collective-permute-start | bytes 258056 | tf_op jit(solution)/shard_map/ppermute | solution.py:217
  32.4 5.4 %collective-permute-start.11 = (bf16[4,5376]{1,0:T(4,128)(2,1)S(1)}, bf16[4,5376]{1,0:T(4,128)(2,1)S(1)}, u32[]{:S(2)}, u32[]{:S(2)}) collective-permute-start(bf16[4,5376]{1,0:T(4,128)(2,1)S(1)} %get-tuple-element.36), channel_id=1, source_target_pairs={{0,8},{1,9},{2,10},{3,11},{4,12},{5,13},{6,14},{7,15},{8,0},{9,1},... | collective-permute-start | bytes 129032 | tf_op jit(solution)/shard_map/ppermute | solution.py:217

commit v3 on v2

--- a/solution.py
+++ b/solution.py
@@ -105,15 +105,15 @@
     if not coded:
         return ref[:, width : width + HDIM], ref[:, width + HDIM :], None
     maxima, denominators, unit = unpack_statistics(ref[:, width:], width // HDIM)
-    return maxima, denominators, unit * (1.0 / CODE_SPAN)
+    return maxima, denominators, unit * (1.0 / CODE_SPAN**2)
 
 
 def read_numerator(ref, columns, coded):
     if not coded:
         return ref[:, columns]
     code = ref[:, columns].astype(jnp.float32)
-    size = jnp.log2(jnp.abs(code)) + CODE_SPAN / 2
-    return jnp.where(code < 0, -size, size)
+    root = jnp.log2(jnp.abs(code)) + CODE_SPAN / 2
+    return jnp.where(code < 0, -root, root) * root
 
 
 def combine(refs, coded, width):
@@ -153,7 +153,7 @@
     combined = [combine(group, kinds, width) for group in sources]
     steps = []
     for index, (group, keep_ref, (maxima, denominators, factors)) in enumerate(zip(sources, keeps, combined)):
-        largest = jnp.full((sent, HDIM), 1e-30, jnp.float32)
+        largest = jnp.full((sent, HDIM), 1e-32, jnp.float32)
         for head in range(heads):
             columns = slice(head * HDIM, (head + 1) * HDIM)
             merged = combined_mean(group, kinds, factors, head)
@@ -164,7 +164,7 @@
         keep_ref[:, width + HDIM :] = denominators[:block]
         unit = jnp.broadcast_to(jnp.max(largest, axis=1, keepdims=True), largest.shape)
         unit = (unit * 1.01).astype(jnp.bfloat16).astype(jnp.float32)
-        steps.append((CODE_SPAN / unit, pack_statistics(maxima[block:], denominators[block:], unit, heads)))
+        steps.append((CODE_SPAN**2 / unit, pack_statistics(maxima[block:], denominators[block:], unit, heads)))
     for index, (chain, (step, statistics)) in enumerate(zip(chains, steps)):
         for place, all_send_ref in enumerate(all_send_refs):
             rows = slice(place * block, (place + 1) * block)
@@ -173,7 +173,8 @@
             for head in range(heads):
                 columns = slice(head * HDIM, (head + 1) * HDIM)
                 mean = means_ref[rows, index * width + head * HDIM : index * width + (head + 1) * HDIM]
-                code = jnp.exp2(jnp.abs(mean) * step[rows] - CODE_SPAN / 2)
+                square = jnp.abs(mean) * step[rows]
+                code = jnp.exp2(square * lax.rsqrt(jnp.maximum(square, 1e-30)) - CODE_SPAN / 2)
                 send_ref[:, columns] = jnp.where(mean < 0, -code, code).astype(jnp.bfloat16)
 
 
@@ -219,7 +220,7 @@
 
 def chip_stages(peers):
     bits = [1 << bit for bit in range(1, peers.bit_length() - 1)]
-    square = [bits[:1], [sum(bits[:2]), *bits[:2]]][len(bits) > 2]
+    square = [bits[:1], [bits[0], sum(bits[:2]), bits[1]]][len(bits) > 2]
     return [square, *([bit] for bit in bits[len(square).bit_length() :])]
 
 

time: 39 us -> 37.4 us (0.959)
  waiting for transfers between devices: 16.2 us -> 14.5 us
    ppermute x12, waiting for transfers between devices: 16.2 us -> 14.5 us  [exchange(): lax.ppermute(array, 'seq', [(i, i ^ mask) for i in range(lax.axis_size('s...]
  transfers between devices with their start and end apart: 12 -> 12, of which waited for: 10 -> 10; matrix products, arithmetic and copies ran while one was open for 0% -> 0% of each run, Pallas kernels for 11% -> 12%
where the time goes in v3:
time: 37.4 us; the launch traced here: 37.3 us
  starting transfers between devices  15.4 us (41%)
  waiting for transfers between devices  14.5 us (39%)
  Pallas kernels  6.5 us (17%)
  local copies, waits for them, and re-layouts  0.79 us (2%)
    ppermute x12, starting transfers between devices, exchange(): lax.ppermute(array, 'seq', [(i, i ^ mask) for i in range(lax.axis_size('s...  15.4 us
    ppermute x12, waiting for transfers between devices, exchange(): lax.ppermute(array, 'seq', [(i, i ^ mask) for i in range(lax.axis_size('s...  14.5 us
    pallas_call x9, Pallas kernels, call(): pl.pallas_call(kernel, out_shape=out_shape, in_specs=[VMEM_SPEC] * len(op...  6.5 us
    unnamed x8, local copies, waits for them, and re-layouts  0.79 us
  transfers between devices with their start and end apart: 12, of which 10 were waited for; matrix products, arithmetic and copies ran while one was open for 0% of the time, Pallas kernels for 12%

profile of v3, /device:TPU:0, one launch (start us, length us, event | category | flops | bytes accessed | tf_op | source)
XLA Modules:
  0.0 37.3 jit_solution(5223137137298630133)
XLA Ops:
  0.0 4.1 %collective-permute-start = (bf16[4,5120]{1,0:T(4,128)(2,1)}, bf16[4,5120]{1,0:T(4,128)(2,1)S(1)}, u32[]{:S(2)}, u32[]{:S(2)}) collective-permute-start(bf16[4,5120]{1,0:T(4,128)(2,1)} %refs_0_.1), channel_id=1, source_target_pairs={{0,8},{1,9},{2,10},{3,11},{4,12},{5,13},{6,14},{7,15},{8,0},{9,1},... | collective-permute-start | bytes 122888 | tf_op jit(solution)/shard_map/ppermute | solution.py:218
  4.1 2.6 %collective-permute-done.refs_1_ = bf16[4,5120]{1,0:T(4,128)(2,1)S(1)} collective-permute-done((bf16[4,5120]{1,0:T(4,128)(2,1)}, bf16[4,5120]{1,0:T(4,128)(2,1)S(1)}, u32[]{:S(2)}, u32[]{:S(2)}) %collective-permute-start) | collective-permute-done | bytes 40992 | tf_op jit(solution)/shard_map/ppermute | solution.py:218
  6.7 0.8 %copy-done.2 = bf16[4,5120]{1,0:T(4,128)(2,1)S(1)} copy-done((bf16[4,5120]{1,0:T(4,128)(2,1)S(1)}, bf16[4,5120]{1,0:T(4,128)(2,1)}, u32[]{:S(2)}) %copy-start.2) | copy-done | bytes 40984
  7.5 1.8 %collective-permute-start.1 = (bf16[8,5120]{1,0:T(8,128)(2,1)S(1)}, bf16[8,5120]{1,0:T(8,128)(2,1)S(1)}, u32[]{:S(2)}, u32[]{:S(2)}) collective-permute-start(bf16[8,5120]{1,0:T(8,128)(2,1)S(1)} %shard_map.46.refs_0_), channel_id=1, source_target_pairs={{0,2},{1,3},{2,0},{3,1},{4,6},{5,7},{6,4},{7,5},{8,10},{9,11},{10,... | collective-permute-start | bytes 245768 | tf_op jit(solution)/shard_map/ppermute | solution.py:218
  9.3 1.2 %collective-permute-start.2 = (bf16[8,5120]{1,0:T(8,128)(2,1)S(1)}, bf16[8,5120]{1,0:T(8,128)(2,1)S(1)}, u32[]{:S(2)}, u32[]{:S(2)}) collective-permute-start(bf16[8,5120]{1,0:T(8,128)(2,1)S(1)} %shard_map.46.refs_0_), channel_id=1, source_target_pairs={{0,6},{1,7},{2,4},{3,5},{4,2},{5,3},{6,0},{7,1},{8,14},{9,15},{10,... | collective-permute-start | bytes 245768 | tf_op jit(solution)/shard_map/ppermute | solution.py:218
  10.5 0.6 %collective-permute-start.3 = (bf16[8,5120]{1,0:T(8,128)(2,1)S(1)}, bf16[8,5120]{1,0:T(8,128)(2,1)S(1)}, u32[]{:S(2)}, u32[]{:S(2)}) collective-permute-start(bf16[8,5120]{1,0:T(8,128)(2,1)S(1)} %shard_map.46.refs_0_), channel_id=1, source_target_pairs={{0,4},{1,5},{2,6},{3,7},{4,0},{5,1},{6,2},{7,3},{8,12},{9,13},{10,... | collective-permute-start | bytes 245768 | tf_op jit(solution)/shard_map/ppermute | solution.py:218
  11.1 1.6 %collective-permute-done.1.refs_1_ = bf16[8,5120]{1,0:T(8,128)(2,1)S(1)} collective-permute-done((bf16[8,5120]{1,0:T(8,128)(2,1)S(1)}, bf16[8,5120]{1,0:T(8,128)(2,1)S(1)}, u32[]{:S(2)}, u32[]{:S(2)}) %collective-permute-start.1) | collective-permute-done | bytes 81952 | tf_op jit(solution)/shard_map/ppermute | solution.py:218
  12.6 2.0 %collective-permute-done.2.refs_2_ = bf16[8,5120]{1,0:T(8,128)(2,1)S(1)} collective-permute-done((bf16[8,5120]{1,0:T(8,128)(2,1)S(1)}, bf16[8,5120]{1,0:T(8,128)(2,1)S(1)}, u32[]{:S(2)}, u32[]{:S(2)}) %collective-permute-start.2) | collective-permute-done | bytes 81952 | tf_op jit(solution)/shard_map/ppermute | solution.py:218
  15.1 0.5 %collective-permute-start.4 = (bf16[32,2560]{1,0:T(8,128)(2,1)S(1)}, bf16[32,2560]{1,0:T(8,128)(2,1)S(1)}, u32[]{:S(2)}, u32[]{:S(2)}) collective-permute-start(bf16[32,2560]{1,0:T(8,128)(2,1)S(1)} %get-tuple-element.21.query_here_ref), channel_id=1, source_target_pairs={{0,1},{1,0},{2,3},{3,2},{4,5},{5,4},{6,7},{7,6},{8,9},{9,8},{10,11... | collective-permute-start | bytes 491528 | tf_op jit(solution)/shard_map/ppermute | solution.py:218
  15.6 0.9 %collective-permute-done.6.query_there_ref = bf16[32,2560]{1,0:T(8,128)(2,1)S(1)} collective-permute-done((bf16[32,2560]{1,0:T(8,128)(2,1)S(1)}, bf16[32,2560]{1,0:T(8,128)(2,1)S(1)}, u32[]{:S(2)}, u32[]{:S(2)}) %collective-permute-start.6) | collective-permute-done | bytes 163872 | tf_op jit(solution)/shard_map/ppermute | solution.py:218
  16.5 2.0 %shard_map.49 = (f32[32,2816]{1,0:T(8,128)S(1)}, f32[32,2816]{1,0:T(8,128)S(1)}) custom-call(bf16[32,2560]{1,0:T(8,128)(2,1)S(1)} %get-tuple-element.24.query_here_ref, bf16[32,2560]{1,0:T(8,128)(2,1)S(1)} %collective-permute-done.6.query_there_ref, bf16[512,5120]{1,0:T(8,128)(2,1)S(1)} %copy-done, bf16[512,5120]{1,0:T(8,128)(2,1)S(1)} %copy-done.1), custom_call_target="tpu_custom_call" | custom-call | flops 335544320 | bytes 11534336 | tf_op jit(solution)/shard_map/pallas_call | solution.py:205
  18.6 1.9 %shard_map.48 = (f32[32,2816]{1,0:T(8,128)S(1)}, f32[32,2816]{1,0:T(8,128)S(1)}) custom-call(bf16[32,2560]{1,0:T(8,128)(2,1)S(1)} %get-tuple-element.21.query_here_ref, bf16[32,2560]{1,0:T(8,128)(2,1)S(1)} %collective-permute-done.4.query_there_ref, bf16[512,5120]{1,0:T(8,128)(2,1)S(1)} %copy-done, bf16[512,5120]{1,0:T(8,128)(2,1)S(1)} %copy-done.1), custom_call_target="tpu_custom_call" | custom-call | flops 335544320 | bytes 11534336 | tf_op jit(solution)/shard_map/pallas_call | solution.py:205
  21.0 0.5 %shard_map.50 = (f32[8,5632]{1,0:T(8,128)S(1)}, bf16[8,5376]{1,0:T(8,128)(2,1)S(1)}, bf16[8,5376]{1,0:T(8,128)(2,1)S(1)}, bf16[8,5376]{1,0:T(8,128)(2,1)S(1)}) custom-call(f32[32,2816]{1,0:T(8,128)S(1)} %get-tuple-element.25.refs_0_, f32[32,2816]{1,0:T(8,128)S(1)} %collective-permute-done.7.refs_1_), custom_call_target="tpu_custom_call" | custom-call | bytes 1159168 | tf_op jit(solution)/shard_map/pallas_call | solution.py:205
  21.5 0.8 %collective-permute-done.5.refs_1_ = f32[32,2816]{1,0:T(8,128)S(1)} collective-permute-done((f32[32,2816]{1,0:T(8,128)S(1)}, f32[32,2816]{1,0:T(8,128)S(1)}, u32[]{:S(2)}, u32[]{:S(2)}) %collective-permute-start.5) | collective-permute-done | bytes 360480 | tf_op jit(solution)/shard_map/ppermute | solution.py:218
  22.8 1.0 %collective-permute-start.10 = (bf16[8,5376]{1,0:T(8,128)(2,1)S(1)}, bf16[8,5376]{1,0:T(8,128)(2,1)S(1)}, u32[]{:S(2)}, u32[]{:S(2)}) collective-permute-start(bf16[8,5376]{1,0:T(8,128)(2,1)S(1)} %get-tuple-element.34), channel_id=1, source_target_pairs={{0,4},{1,5},{2,6},{3,7},{4,0},{5,1},{6,2},{7,3},{8,12},{9,13},{10,... | collective-permute-start | bytes 258056 | tf_op jit(solution)/shard_map/ppermute | solution.py:218
  23.8 1.4 %collective-permute-start.8 = (bf16[8,5376]{1,0:T(8,128)(2,1)S(1)}, bf16[8,5376]{1,0:T(8,128)(2,1)S(1)}, u32[]{:S(2)}, u32[]{:S(2)}) collective-permute-start(bf16[8,5376]{1,0:T(8,128)(2,1)S(1)} %get-tuple-element.32), channel_id=1, source_target_pairs={{0,2},{1,3},{2,0},{3,1},{4,6},{5,7},{6,4},{7,5},{8,10},{9,11},{10,... | collective-permute-start | bytes 258056 | tf_op jit(solution)/shard_map/ppermute | solution.py:218
  25.3 1.1 %collective-permute-start.9 = (bf16[8,5376]{1,0:T(8,128)(2,1)S(1)}, bf16[8,5376]{1,0:T(8,128)(2,1)S(1)}, u32[]{:S(2)}, u32[]{:S(2)}) collective-permute-start(bf16[8,5376]{1,0:T(8,128)(2,1)S(1)} %get-tuple-element.33), channel_id=1, source_target_pairs={{0,6},{1,7},{2,4},{3,5},{4,2},{5,3},{6,0},{7,1},{8,14},{9,15},{10,... | collective-permute-start | bytes 258056 | tf_op jit(solution)/shard_map/ppermute | solution.py:218
  26.4 1.3 %collective-permute-done.10.refs_3_ = bf16[8,5376]{1,0:T(8,128)(2,1)S(1)} collective-permute-done((bf16[8,5376]{1,0:T(8,128)(2,1)S(1)}, bf16[8,5376]{1,0:T(8,128)(2,1)S(1)}, u32[]{:S(2)}, u32[]{:S(2)}) %collective-permute-start.10) | collective-permute-done | bytes 86048 | tf_op jit(solution)/shard_map/ppermute | solution.py:218
  27.7 1.5 %collective-permute-done.8.refs_1_ = bf16[8,5376]{1,0:T(8,128)(2,1)S(1)} collective-permute-done((bf16[8,5376]{1,0:T(8,128)(2,1)S(1)}, bf16[8,5376]{1,0:T(8,128)(2,1)S(1)}, u32[]{:S(2)}, u32[]{:S(2)}) %collective-permute-start.8) | collective-permute-done | bytes 86048 | tf_op jit(solution)/shard_map/ppermute | solution.py:218
  29.2 1.5 %collective-permute-done.9.refs_2_ = bf16[8,5376]{1,0:T(8,128)(2,1)S(1)} collective-permute-done((bf16[8,5376]{1,0:T(8,128)(2,1)S(1)}, bf16[8,5376]{1,0:T(8,128)(2,1)S(1)}, u32[]{:S(2)}, u32[]{:S(2)}) %collective-permute-start.9) | collective-permute-done | bytes 86048 | tf_op jit(solution)/shard_map/ppermute | solution.py:218
  30.6 0.6 %shard_map.52 = (f32[4,5632]{1,0:T(4,128)S(1)}, bf16[4,5376]{1,0:T(4,128)(2,1)S(1)}) custom-call(f32[8,5632]{1,0:T(8,128)S(1)} %get-tuple-element.31.refs_0_, bf16[8,5376]{1,0:T(8,128)(2,1)S(1)} %collective-permute-done.8.refs_1_, bf16[8,5376]{1,0:T(8,128)(2,1)S(1)} %collective-permute-done.9.refs_2_, bf16[8,5376]{1,0:T(8,128)(2,1)S(1)} %collective-permute-done.10.refs_3_), custom_call_target="tpu_custom_call" | custom-call | bytes 571392 | tf_op jit(solution)/shard_map/pallas_call | solution.py:205
  31.2 3.0 %collective-permute-start.11 = (bf16[4,5376]{1,0:T(4,128)(2,1)S(1)}, bf16[4,5376]{1,0:T(4,128)(2,1)S(1)}, u32[]{:S(2)}, u32[]{:S(2)}) collective-permute-start(bf16[4,5376]{1,0:T(4,128)(2,1)S(1)} %get-tuple-element.36), channel_id=1, source_target_pairs={{0,8},{1,9},{2,10},{3,11},{4,12},{5,13},{6,14},{7,15},{8,0},{9,1},... | collective-permute-start | bytes 129032 | tf_op jit(solution)/shard_map/ppermute | solution.py:218
  34.2 2.0 %collective-permute-done.11.refs_1_ = bf16[4,5376]{1,0:T(4,128)(2,1)S(1)} collective-permute-done((bf16[4,5376]{1,0:T(4,128)(2,1)S(1)}, bf16[4,5376]{1,0:T(4,128)(2,1)S(1)}, u32[]{:S(2)}, u32[]{:S(2)}) %collective-permute-start.11) | collective-permute-done | bytes 43040 | tf_op jit(solution)/shard_map/ppermute | solution.py:218
  36.2 1.0 %shard_map.54 = bf16[4,5120]{1,0:T(4,128)(2,1)} custom-call(f32[4,5632]{1,0:T(4,128)S(1)} %get-tuple-element.35.refs_0_, bf16[4,5376]{1,0:T(4,128)(2,1)S(1)} %collective-permute-done.11.refs_1_, f32[1,5120]{1,0:T(1,128)S(1)} %shard_map.53.refs_2_), custom_call_target="tpu_custom_call" | custom-call | bytes 194560 | tf_op jit(solution)/shard_map/pallas_call | solution.py:205
  (17 shorter events, 1.6 us)
Async XLA Ops:
  0.0 16.5 %copy-start = (bf16[512,5120]{1,0:T(8,128)(2,1)S(1)}, bf16[512,5120]{1,0:T(8,128)(2,1)}, u32[]{:S(2)}) copy-start(bf16[512,5120]{1,0:T(8,128)(2,1)} %key_ref.3) | copy-start | bytes 15728644
  0.0 16.5 %copy-start.1 = (bf16[512,5120]{1,0:T(8,128)(2,1)S(1)}, bf16[512,5120]{1,0:T(8,128)(2,1)}, u32[]{:S(2)}) copy-start(bf16[512,5120]{1,0:T(8,128)(2,1)} %value_ref.3) | copy-start | bytes 15728644
  0.0 6.7 %collective-permute-start = (bf16[4,5120]{1,0:T(4,128)(2,1)}, bf16[4,5120]{1,0:T(4,128)(2,1)S(1)}, u32[]{:S(2)}, u32[]{:S(2)}) collective-permute-start(bf16[4,5120]{1,0:T(4,128)(2,1)} %refs_0_.1), channel_id=1, source_target_pairs={{0,8},{1,9},{2,10},{3,11},{4,12},{5,13},{6,14},{7,15},{8,0},{9,1},... | collective-permute-start | bytes 122888 | tf_op jit(solution)/shard_map/ppermute | solution.py:218
  6.7 0.8 %copy-start.2 = (bf16[4,5120]{1,0:T(4,128)(2,1)S(1)}, bf16[4,5120]{1,0:T(4,128)(2,1)}, u32[]{:S(2)}) copy-start(bf16[4,5120]{1,0:T(4,128)(2,1)} %refs_0_.1) | copy-start | bytes 122884
  7.5 5.1 %collective-permute-start.1 = (bf16[8,5120]{1,0:T(8,128)(2,1)S(1)}, bf16[8,5120]{1,0:T(8,128)(2,1)S(1)}, u32[]{:S(2)}, u32[]{:S(2)}) collective-permute-start(bf16[8,5120]{1,0:T(8,128)(2,1)S(1)} %shard_map.46.refs_0_), channel_id=1, source_target_pairs={{0,2},{1,3},{2,0},{3,1},{4,6},{5,7},{6,4},{7,5},{8,10},{9,11},{10,... | collective-permute-start | bytes 245768 | tf_op jit(solution)/shard_map/ppermute | solution.py:218
  9.3 5.3 %collective-permute-start.2 = (bf16[8,5120]{1,0:T(8,128)(2,1)S(1)}, bf16[8,5120]{1,0:T(8,128)(2,1)S(1)}, u32[]{:S(2)}, u32[]{:S(2)}) collective-permute-start(bf16[8,5120]{1,0:T(8,128)(2,1)S(1)} %shard_map.46.refs_0_), channel_id=1, source_target_pairs={{0,6},{1,7},{2,4},{3,5},{4,2},{5,3},{6,0},{7,1},{8,14},{9,15},{10,... | collective-permute-start | bytes 245768 | tf_op jit(solution)/shard_map/ppermute | solution.py:218
  10.5 4.4 %collective-permute-start.3 = (bf16[8,5120]{1,0:T(8,128)(2,1)S(1)}, bf16[8,5120]{1,0:T(8,128)(2,1)S(1)}, u32[]{:S(2)}, u32[]{:S(2)}) collective-permute-start(bf16[8,5120]{1,0:T(8,128)(2,1)S(1)} %shard_map.46.refs_0_), channel_id=1, source_target_pairs={{0,4},{1,5},{2,6},{3,7},{4,0},{5,1},{6,2},{7,3},{8,12},{9,13},{10,... | collective-permute-start | bytes 245768 | tf_op jit(solution)/shard_map/ppermute | solution.py:218
  15.0 1.5 %collective-permute-start.6 = (bf16[32,2560]{1,0:T(8,128)(2,1)S(1)}, bf16[32,2560]{1,0:T(8,128)(2,1)S(1)}, u32[]{:S(2)}, u32[]{:S(2)}) collective-permute-start(bf16[32,2560]{1,0:T(8,128)(2,1)S(1)} %get-tuple-element.24.query_here_ref), channel_id=1, source_target_pairs={{0,1},{1,0},{2,3},{3,2},{4,5},{5,4},{6,7},{7,6},{8,9},{9,8},{10,11... | collective-permute-start | bytes 491528 | tf_op jit(solution)/shard_map/ppermute | solution.py:218
  15.1 3.6 %collective-permute-start.4 = (bf16[32,2560]{1,0:T(8,128)(2,1)S(1)}, bf16[32,2560]{1,0:T(8,128)(2,1)S(1)}, u32[]{:S(2)}, u32[]{:S(2)}) collective-permute-start(bf16[32,2560]{1,0:T(8,128)(2,1)S(1)} %get-tuple-element.21.query_here_ref), channel_id=1, source_target_pairs={{0,1},{1,0},{2,3},{3,2},{4,5},{5,4},{6,7},{7,6},{8,9},{9,8},{10,11... | collective-permute-start | bytes 491528 | tf_op jit(solution)/shard_map/ppermute | solution.py:218
  18.4 15.8 %copy-start.3 = (f32[5120]{0:T(1024)S(1)}, f32[5120]{0:T(1024)}, u32[]{:S(2)}) copy-start(f32[5120]{0:T(1024)} %param.7) | copy-start | bytes 61444
  18.4 2.6 %collective-permute-start.7 = (f32[32,2816]{1,0:T(8,128)S(1)}, f32[32,2816]{1,0:T(8,128)S(1)}, u32[]{:S(2)}, u32[]{:S(2)}) collective-permute-start(f32[32,2816]{1,0:T(8,128)S(1)} %get-tuple-element.26), channel_id=1, source_target_pairs={{0,1},{1,0},{2,3},{3,2},{4,5},{5,4},{6,7},{7,6},{8,9},{9,8},{10,11... | collective-permute-start | bytes 1081352 | tf_op jit(solution)/shard_map/ppermute | solution.py:218
  20.6 1.7 %collective-permute-start.5 = (f32[32,2816]{1,0:T(8,128)S(1)}, f32[32,2816]{1,0:T(8,128)S(1)}, u32[]{:S(2)}, u32[]{:S(2)}) collective-permute-start(f32[32,2816]{1,0:T(8,128)S(1)} %get-tuple-element.23), channel_id=1, source_target_pairs={{0,1},{1,0},{2,3},{3,2},{4,5},{5,4},{6,7},{7,6},{8,9},{9,8},{10,11... | collective-permute-start | bytes 1081352 | tf_op jit(solution)/shard_map/ppermute | solution.py:218
  22.8 4.9 %collective-permute-start.10 = (bf16[8,5376]{1,0:T(8,128)(2,1)S(1)}, bf16[8,5376]{1,0:T(8,128)(2,1)S(1)}, u32[]{:S(2)}, u32[]{:S(2)}) collective-permute-start(bf16[8,5376]{1,0:T(8,128)(2,1)S(1)} %get-tuple-element.34), channel_id=1, source_target_pairs={{0,4},{1,5},{2,6},{3,7},{4,0},{5,1},{6,2},{7,3},{8,12},{9,13},{10,... | collective-permute-start | bytes 258056 | tf_op jit(solution)/shard_map/ppermute | solution.py:218
  23.8 5.4 %collective-permute-start.8 = (bf16[8,5376]{1,0:T(8,128)(2,1)S(1)}, bf16[8,5376]{1,0:T(8,128)(2,1)S(1)}, u32[]{:S(2)}, u32[]{:S(2)}) collective-permute-start(bf16[8,5376]{1,0:T(8,128)(2,1)S(1)} %get-tuple-element.32), channel_id=1, source_target_pairs={{0,2},{1,3},{2,0},{3,1},{4,6},{5,7},{6,4},{7,5},{8,10},{9,11},{10,... | collective-permute-start | bytes 258056 | tf_op jit(solution)/shard_map/ppermute | solution.py:218
  25.3 5.4 %collective-permute-start.9 = (bf16[8,5376]{1,0:T(8,128)(2,1)S(1)}, bf16[8,5376]{1,0:T(8,128)(2,1)S(1)}, u32[]{:S(2)}, u32[]{:S(2)}) collective-permute-start(bf16[8,5376]{1,0:T(8,128)(2,1)S(1)} %get-tuple-element.33), channel_id=1, source_target_pairs={{0,6},{1,7},{2,4},{3,5},{4,2},{5,3},{6,0},{7,1},{8,14},{9,15},{10,... | collective-permute-start | bytes 258056 | tf_op jit(solution)/shard_map/ppermute | solution.py:218
  31.2 5.0 %collective-permute-start.11 = (bf16[4,5376]{1,0:T(4,128)(2,1)S(1)}, bf16[4,5376]{1,0:T(4,128)(2,1)S(1)}, u32[]{:S(2)}, u32[]{:S(2)}) collective-permute-start(bf16[4,5376]{1,0:T(4,128)(2,1)S(1)} %get-tuple-element.36), channel_id=1, source_target_pairs={{0,8},{1,9},{2,10},{3,11},{4,12},{5,13},{6,14},{7,15},{8,0},{9,1},... | collective-permute-start | bytes 129032 | tf_op jit(solution)/shard_map/ppermute | solution.py:218
